TPU v7x, 32 devices: a whole 2x2x4 slice. The times are simulated.
32 devices in a mesh: seq: 16 (over z, y, x), head: 2 (over core).
Axes of the slice: x: 2, y: 2, z: 4, core: 2. Of those that a mesh axis runs over, the one named last changes fastest.
Arguments:
- queries: bfloat16 [16384, 32, 128], P('seq', 'head'), may hold values from -6 to 6
- key_rows: bfloat16 [16384, 32, 128], P('seq', 'head'), may hold values from -6 to 6
- value_rows: bfloat16 [16384, 32, 128], P('seq', 'head'), may hold values from -6 to 6
- level_weights: float32 [7, 32, 16384], P(None, 'head', 'seq'), may hold values from 0.2 to 30
- out_gain: float32 [32, 128], P('head'), may hold values from 0.25 to 1.75
Outputs:
- attended: bfloat16 [16384, 32, 128], P('seq', 'head')
All inputs are finite; a program needn't handle non-finite values.
Results may differ from a plain program's by a relative error of at most 0.0062.
Values may be sent and summed in bfloat16 or wider, within the bound.
A program may use at most 192 MiB of HBM per device.

v0:
```python
import math

import jax
import jax.numpy as jnp
import numpy as np
from jax import lax
from jax.sharding import PartitionSpec as P

HEADS = 32
HEAD_DIM = 128
STRETCH = 256


def shifted(x, axis, by):
    devices = lax.axis_size(axis)
    pairs = [(i, i + by) for i in range(devices) if 0 <= i + by < devices]
    return lax.ppermute(x, axis, pairs)


def inner_selector(block_count, inner_bits):
    table = np.zeros((block_count, max(inner_bits - 1, 0), block_count), np.float32)
    for target in range(block_count):
        for source in range(target - 1):
            highest = (target ^ source).bit_length() - 1
            table[target, highest - 1, source] = 1.0
    return table


def on_device(queries, key_rows, value_rows, level_weights, out_gain):
    tok_count, head_count, head_width = queries.shape
    level_count = level_weights.shape[0]
    block_count = tok_count // STRETCH
    inner_bits = block_count.bit_length() - 1
    seq_bits = lax.axis_size("seq").bit_length() - 1
    seq_index = lax.axis_index("seq")
    score_scale = 1.0 / math.sqrt(head_width)
    query_blocks = queries.reshape(block_count, STRETCH, head_count, head_width)
    key_blocks = key_rows.reshape(block_count, STRETCH, head_count, head_width)
    value_blocks = value_rows.reshape(block_count, STRETCH, head_count, head_width)
    last_pair = jnp.stack([key_rows[tok_count - STRETCH :], value_rows[tok_count - STRETCH :]])
    arrived = shifted(last_pair, "seq", 1)
    halo_keys = arrived[0]
    halo_values = arrived[1]
    prev_keys = jnp.concatenate([halo_keys[None], key_blocks[:-1]], 0)
    prev_values = jnp.concatenate([halo_values[None], value_blocks[:-1]], 0)
    positions = jnp.arange(STRETCH)
    causal = positions[:, None] >= positions[None, :]
    own_scores = (
        jnp.einsum("cthd,cuhd->chtu", query_blocks, key_blocks, preferred_element_type=jnp.float32)
        * score_scale
    )
    own_scores = jnp.where(causal, own_scores, 0.0).astype(jnp.bfloat16)
    prev_scores = (
        jnp.einsum("cthd,cuhd->chtu", query_blocks, prev_keys, preferred_element_type=jnp.float32)
        * score_scale
    ).astype(jnp.bfloat16)
    own_part = jnp.einsum(
        "chtu,cuhd->cthd", own_scores, value_blocks, preferred_element_type=jnp.float32
    )
    prev_part = jnp.einsum(
        "chtu,cuhd->cthd", prev_scores, prev_values, preferred_element_type=jnp.float32
    )
    block_states = jnp.einsum(
        "cuhd,cuhe->chde", key_blocks, value_blocks, preferred_element_type=jnp.float32
    )
    halo_state = jnp.einsum(
        "uhd,uhe->hde", halo_keys, halo_values, preferred_element_type=jnp.float32
    )
    device_total = jnp.sum(block_states, 0).astype(jnp.bfloat16)
    piece = lax.all_gather(device_total[None], "seq", axis=0, tiled=True)
    sources = jnp.arange(piece.shape[0], dtype=jnp.int32)
    selector_rows = []
    for add_level_bit in range(seq_bits):
        same_above = sources >> add_level_bit + 1 == seq_index >> add_level_bit + 1
        source_low = sources >> add_level_bit & 1 == 0
        target_high = seq_index >> add_level_bit & 1 == 1
        selector_rows.append((same_above & source_low & target_high).astype(jnp.bfloat16))
    selector = jnp.stack(selector_rows)
    group_sums = jnp.einsum("ln,nhde->lhde", selector, piece, preferred_element_type=jnp.float32)
    inner_states = jnp.einsum(
        "cbj,jhde->cbhde",
        jnp.asarray(inner_selector(block_count, inner_bits)),
        block_states,
        precision=lax.Precision.HIGHEST,
    )
    lowest_flags = jnp.stack(
        [
            ((seq_index >> level_bit & 1 == 1) & (seq_index & (1 << level_bit) - 1 == 0)).astype(
                jnp.float32
            )
            for level_bit in range(seq_bits)
        ]
    )
    first_block = (jnp.arange(block_count) == 0).astype(jnp.float32)
    correction = lowest_flags[:, None, None, None] * halo_state[None]
    outer_states = group_sums[None] - first_block[:, None, None, None, None] * correction[None]
    far_states = jnp.concatenate([inner_states, outer_states], 1).astype(jnp.bfloat16)
    weight_blocks = jnp.transpose(
        level_weights.reshape(level_count, head_count, block_count, STRETCH), (2, 3, 1, 0)
    )
    scaled = (
        query_blocks[:, :, :, None, :] * weight_blocks[:, :, :, 2:, None] * score_scale
    ).astype(jnp.bfloat16)
    far_part = jnp.einsum(
        "cthld,clhde->cthe", scaled, far_states, preferred_element_type=jnp.float32
    )
    mixed_out = (
        weight_blocks[:, :, :, 0:1] * own_part + weight_blocks[:, :, :, 1:2] * prev_part + far_part
    )
    mixed_out = mixed_out.reshape(tok_count, head_count, head_width)
    square_sum = jnp.sum(mixed_out * mixed_out, axis=(1, 2))
    whole_sum = lax.psum(square_sum, "head")
    inverse = lax.rsqrt(whole_sum / (HEADS * HEAD_DIM) + 1e-06)
    return (mixed_out * inverse[:, None, None] * out_gain[None]).astype(jnp.bfloat16)


def solution(mesh):
    placed = (
        P("seq", "head", None),
        P("seq", "head", None),
        P("seq", "head", None),
        P(None, "head", "seq"),
        P("head", None),
    )
    return jax.shard_map(
        on_device, mesh=mesh, in_specs=placed, out_specs=P("seq", "head", None), check_vma=False
    )
```

profile of v0, /device:TPU:0, one launch (start us, length us, event | category | flops | bytes accessed | tf_op | source)
XLA Modules:
  0.0 260.6 jit_solution(8570998202023379817)
XLA Ops:
  6.5 0.0 all-gather.3.cloned.1.call-start
  6.5 7.5 %copy.67 = bf16[4,256,16,128]{1,3,2,0:T(8,128)(2,1)} copy(bf16[4,256,16,128]{3,2,1,0:T(8,128)(2,1)} %bitcast.73) | data formatting | bytes 8388608 | tf_op jit(solution)/shard_map/reshape | solution.py:38
  14.0 7.9 %fusion.62 = (bf16[16,128,128]{2,1,0:T(8,128)(2,1)}, f32[4,16,128,128]{3,2,1,0:T(8,128)}) fusion(bf16[4,256,16,128]{1,3,2,0:T(8,128)(2,1)} %copy.67, bf16[4,256,16,128]{3,2,1,0:T(8,128)(2,1)} %bitcast.71), kind=kOutput, calls=%fused_computation.75 | convolution fusion | flops 537657344 | bytes 13107200 | tf_op jit(solution)/shard_map/cuhd,cuhe->chde/dot_general | solution.py:63
  21.9 0.0 all-gather.3.cloned.1.call-update
  21.9 1.4 slice.36
  23.3 1.4 slice.35
  24.7 0.0 copy-start.8
  24.7 0.3 copy.116
  25.0 0.3 copy.117
  25.3 1.5 pad_maximum_fusion
  26.8 6.7 %collective-permute-start = (bf16[2,256,16,128]{3,1,2,0:T(8,128)(2,1)}, bf16[2,256,16,128]{3,1,2,0:T(8,128)(2,1)}, u32[]{:S(2)}, u32[]{:S(2)}) collective-permute-start(bf16[2,256,16,128]{3,1,2,0:T(8,128)(2,1)} %pad_maximum_fusion), channel_id=1, source_target_pairs={{0,2},{2,4},{4,6},{6,8},{8,10},{10,12},{12,14},{14,16},{16,18},{18... | collective-permute-start | bytes 6291464 | tf_op jit(solution)/shard_map/ppermute | solution.py:17
  33.6 0.0 copy-start
  33.6 0.0 copy-done.8
  33.6 13.3 %convert_bitcast_fusion = bf16[4,1,16,128,128]{4,0,3,2,1:T(4,128)(2,1)} fusion(f32[4,4,1,1]{1,0,3,2:T(4,128)S(1)} %copy-done.8, f32[4,16,128,128]{3,2,1,0:T(8,128)} %get-tuple-element.10), kind=kOutput, calls=%fused_computation.38 | convolution fusion | flops 51380224 | bytes 6291520 | tf_op jit(solution)/shard_map/cbj,jhde->cbhde/dot_general | solution.py:80
  46.9 0.0 copy-start.1
  46.9 0.1 add_convert_fusion
  47.0 0.0 copy-done
  47.0 2.2 slice.38
  49.2 1.1 copy-done.1
  50.3 0.5 slice.41
  50.8 4.3 %copy.74 = bf16[4,1,16,128,128]{3,4,1,2,0:T(8,128)(2,1)} copy(bf16[4,1,16,128,128]{4,0,3,2,1:T(4,128)(2,1)} %convert_bitcast_fusion) | data formatting | bytes 4194304 | tf_op jit(solution)/shard_map/cbj,jhde->cbhde/dot_general | solution.py:80
  55.1 0.0 copy-start.6
  55.1 6.6 %copy.75 = f32[4,256,16,128]{3,1,2,0:T(8,128)} copy(bf16[4,256,16,128]{3,2,1,0:T(8,128)(2,1)} %bitcast.77) | data formatting | bytes 12582912 | tf_op jit(solution)/shard_map/convert_element_type | solution.py:102
  61.7 0.0 copy-done.6
  61.7 0.0 copy-start.4
  61.7 0.8 copy-done.4
  62.6 1.0 copy.76
  63.6 5.1 %copy.63 = bf16[3,256,16,128]{1,3,2,0:T(8,128)(2,1)} copy(bf16[3,256,16,128]{3,2,1,0:T(8,128)(2,1)} %bitcast.75) | data formatting | bytes 6291456 | tf_op jit(solution)/shard_map/slice | solution.py:45
  68.7 2.4 copy.64
  71.2 0.9 slice_bitcast_fusion.1
  72.0 12.6 %fusion.27 = f32[4,16,256,128]{3,2,1,0:T(8,128)} fusion(bf16[4,256,16,128]{3,2,1,0:T(8,128)(2,1)} %bitcast.72, bf16[4,256,16,128]{1,3,2,0:T(8,128)(2,1)} %copy.67, pred[256,256]{1,0:T(8,128)(4,1)S(1)} %iota_compare_fusion, bf16[4,256,16,128]{3,2,1,0:T(8,128)(2,1)} %bitcast.78), kind=kOutput, calls=%fused_computation.32 | convolution fusion | flops 2160066560 | bytes 21037056 | tf_op jit(solution)/shard_map/chtu,cuhd->cthd/dot_general | solution.py:57
  84.6 10.9 %collective-permute-done = bf16[2,256,16,128]{3,1,2,0:T(8,128)(2,1)} collective-permute-done((bf16[2,256,16,128]{3,1,2,0:T(8,128)(2,1)}, bf16[2,256,16,128]{3,1,2,0:T(8,128)(2,1)}, u32[]{:S(2)}, u32[]{:S(2)}) %collective-permute-start) | collective-permute-done | bytes 2097184 | tf_op jit(solution)/shard_map/ppermute | solution.py:17
  95.5 2.8 %fusion.61 = (bf16[1,256,16,128]{3,1,2,0:T(8,128)(2,1)S(1)}, bf16[1,256,16,128]{3,1,2,0:T(8,128)(2,1)}) fusion(bf16[2,256,16,128]{3,1,2,0:T(8,128)(2,1)} %collective-permute-done), kind=kLoop, calls=%fused_computation.74 | loop fusion | bytes 4194304 | tf_op jit(solution)/shard_map/slice | solution.py:43
  98.3 1.5 copy.62
  99.9 2.0 fusion.40
  101.9 2.6 broadcast_multiply_fusion
  104.5 62.3 %all-gather.3.cloned.1.call-done = bf16[256,128,128]{2,1,0:T(8,128)(2,1)} async-done(((bf16[16,128,128]{2,1,0:T(8,128)(2,1)}), bf16[256,128,128]{2,1,0:T(8,128)(2,1)}) %all-gather.3.cloned.1.call-update) | async-done | bytes 8388624 | tf_op jit(solution)/shard_map/all_gather | solution.py:70
  166.8 10.4 %fusion.10 = f32[4,16,128,128]{3,0,2,1:T(4,128)} fusion(bf16[16,16,128,128]{3,2,1,0:T(8,128)(2,1)} %bitcast.76, pred[1,16]{1,0:T(4,128)(4,1)S(1)} %get-tuple-element.13, pred[1,16]{1,0:T(4,128)(4,1)S(1)} %get-tuple-element.14, pred[1,16]{1,0:T(4,128)(4,1)S(1)} %get-tuple-element.15, pred[1,16]{1,0:T(4,128)(4,1)S(1)} %get-tuple-element.16), kind=kOutput, calls=%fused_computation.18 | convolution fusion | flops 33554624 | bytes 12582976 | tf_op jit(solution)/shard_map/ln,nhde->lhde/dot_general | solution.py:79
  177.2 5.3 %copy.71 = f32[4,16,128,128]{2,3,0,1:T(8,128)} copy(f32[4,16,128,128]{3,0,2,1:T(4,128)} %fusion.10) | data formatting | bytes 8388608 | tf_op jit(solution)/shard_map/ln,nhde->lhde/dot_general | solution.py:79
  182.5 0.0 copy-start.2
  182.5 9.4 %subtract_convert_fusion = bf16[4,4,16,128,128]{3,4,1,2,0:T(8,128)(2,1)} fusion(f32[4,16,128,128]{2,3,0,1:T(8,128)} %broadcast_multiply_fusion, f32[4]{0:T(128)S(1)} %compare_convert_fusion, f32[4,16,128,128]{2,3,0,1:T(8,128)} %copy.71), kind=kLoop, calls=%fused_computation.5 | loop fusion | flops 12582912 | bytes 16777232 | tf_op jit(solution)/shard_map/convert.7
  191.9 0.0 copy-done.2
  191.9 0.0 copy-start.5
  191.9 5.8 %fusion.73 = bf16[4,5,16,128,128]{3,4,1,2,0:T(8,128)(2,1)S(1)} fusion(bf16[4,4,16,128,128]{3,4,1,2,0:T(8,128)(2,1)} %subtract_convert_fusion, bf16[4,1,16,128,128]{3,4,1,2,0:T(8,128)(2,1)S(1)} %copy-done.2), kind=kLoop, calls=%fused_computation.8.clone.2 | loop fusion | flops 5242880 | bytes 20971520 | tf_op jit(solution)/shard_map/cthld,clhde->cthe/dot_general | solution.py:104
  197.7 0.0 copy-done.5
  197.7 0.0 copy-start.3
  197.7 19.7 %fusion = f32[4,16,128,256,1]{2,3,4,1,0:T(8,128)} fusion(f32[4,256,16,5]{1,3,2,0:T(8,128)S(1)} %copy-done.5, f32[4,256,16,128]{3,1,2,0:T(8,128)} %copy.75, bf16[4,5,16,128,128]{3,4,1,2,0:T(8,128)(2,1)S(1)} %fusion.73), kind=kOutput, calls=%fused_computation.1 | convolution fusion | flops 2715811840 | bytes 27590656 | tf_op jit(solution)/shard_map/cthld,clhde->cthe/dot_general | solution.py:104
  217.4 0.0 copy-done.3
  217.4 15.8 %multiply_reduce_fusion = (f32[4,256]{1,0:T(4,128)S(1)}, f32[4,256,16,128]{3,1,2,0:T(8,128)}) fusion(f32[4,16,128,256,1]{2,3,4,1,0:T(8,128)} %fusion, bf16[3,256,16,128]{3,1,2,0:T(8,128)(2,1)} %copy.64, bf16[1,256,16,128]{3,1,2,0:T(8,128)(2,1)} %get-tuple-element.6, bf16[4,256,16,128]{3,2,1,0:T(8,128)(2,1)} %bitcast.79, ...), kind=kOutput, calls=%fused_computation.20 | convolution fusion | flops 2172648448 | bytes 37883904 | tf_op jit(solution)/shard_map/chtu,cuhd->cthd/dot_general | solution.py:60
  233.2 0.0 copy-start.7
  233.2 11.5 %copy.78 = f32[4,256,16,128]{3,2,1,0:T(8,128)} copy(f32[4,256,16,128]{3,1,2,0:T(8,128)} %get-tuple-element.12) | data formatting | bytes 16777216 | tf_op jit(solution)/shard_map/add | solution.py:108
  244.7 2.4 psum.7
  247.2 0.0 copy-done.7
  247.2 6.4 %fusion.8 = bf16[1024,16,128]{2,1,0:T(8,128)(2,1)} fusion(f32[4,256,16,128]{3,2,1,0:T(8,128)} %copy.78, f32[16,128]{1,0:T(8,128)S(1)} %copy-done.7, f32[1024]{0:T(1024)S(1)} %add_rsqrt_fusion), kind=kLoop, calls=%fused_computation.14 | loop fusion | flops 6291456 | bytes 12595200 | tf_op jit(solution)/shard_map/convert_element_type | solution.py:114
  (8 shorter events, 0.1 us)
Async XLA Ops:
  6.5 160.3 %all-gather.3.cloned.1.call-start = ((), (), s32[]{:S(2)}) async-start(), calls=%async_computation | async-start | bytes 8912896 | tf_op jit(solution)/shard_map/all_gather | solution.py:70
  24.7 8.9 %copy-start.8 = (f32[4,4,1,1]{1,0,3,2:T(4,128)S(1)}, f32[4,4,1,1]{1,0,3,2:T(4,128)}, u32[]{:S(2)}) copy-start(f32[4,4,1,1]{1,0,3,2:T(4,128)} %constant.11) | copy-start | bytes 196
  26.8 68.7 %collective-permute-start = (bf16[2,256,16,128]{3,1,2,0:T(8,128)(2,1)}, bf16[2,256,16,128]{3,1,2,0:T(8,128)(2,1)}, u32[]{:S(2)}, u32[]{:S(2)}) collective-permute-start(bf16[2,256,16,128]{3,1,2,0:T(8,128)(2,1)} %pad_maximum_fusion), channel_id=1, source_target_pairs={{0,2},{2,4},{4,6},{6,8},{8,10},{10,12},{12,14},{14,16},{16,18},{18... | collective-permute-start | bytes 6291464 | tf_op jit(solution)/shard_map/ppermute | solution.py:17
  33.6 13.5 %copy-start = (bf16[1024,16,128]{2,1,0:T(8,128)(2,1)S(1)}, bf16[1024,16,128]{2,1,0:T(8,128)(2,1)}, u32[]{:S(2)}) copy-start(bf16[1024,16,128]{2,1,0:T(8,128)(2,1)} %param.8) | copy-start | bytes 12582916
  46.9 3.3 %copy-start.1 = (bf16[1024,16,128]{2,1,0:T(8,128)(2,1)S(1)}, bf16[1024,16,128]{2,1,0:T(8,128)(2,1)}, u32[]{:S(2)}) copy-start(bf16[1024,16,128]{2,1,0:T(8,128)(2,1)} %param.7) | copy-start | bytes 12582916
  55.1 6.6 %copy-start.6 = (f32[7,16,1024]{2,1,0:T(8,128)S(1)}, f32[7,16,1024]{2,1,0:T(8,128)}, u32[]{:S(2)}) copy-start(f32[7,16,1024]{2,1,0:T(8,128)} %param.9) | copy-start | bytes 1376260
  61.7 0.8 copy-start.4
  182.5 9.4 %copy-start.2 = (bf16[4,1,16,128,128]{3,4,1,2,0:T(8,128)(2,1)S(1)}, bf16[4,1,16,128,128]{3,4,1,2,0:T(8,128)(2,1)}, u32[]{:S(2)}) copy-start(bf16[4,1,16,128,128]{3,4,1,2,0:T(8,128)(2,1)} %copy.74) | copy-start | bytes 6291460
  191.9 5.8 %copy-start.5 = (f32[4,256,16,5]{1,3,2,0:T(8,128)S(1)}, f32[4,256,16,5]{1,3,2,0:T(8,128)}, u32[]{:S(2)}) copy-start(f32[4,256,16,5]{1,3,2,0:T(8,128)} %copy.76) | copy-start | bytes 983044
  197.7 19.7 %copy-start.3 = (bf16[3,256,16,128]{1,3,2,0:T(8,128)(2,1)S(1)}, bf16[3,256,16,128]{1,3,2,0:T(8,128)(2,1)}, u32[]{:S(2)}) copy-start(bf16[3,256,16,128]{1,3,2,0:T(8,128)(2,1)} %copy.63) | copy-start | bytes 9437188
  233.2 14.0 %copy-start.7 = (f32[16,128]{1,0:T(8,128)S(1)}, f32[16,128]{1,0:T(8,128)}, u32[]{:S(2)}) copy-start(f32[16,128]{1,0:T(8,128)} %param.10) | copy-start | bytes 24580
Sparse Core Ops, SparseCore 0:
  22.0 144.7 all-gather.2
where the time goes:
time: 264 us; the launch traced here: 261 us
  matrix products  81.7 us (31%)
  waiting for transfers between devices  73.3 us (28%)
  local copies, waits for them, and re-layouts  56.8 us (22%)
  other arithmetic  25.8 us (10%)
  between operations  13.9 us (5%)
  starting transfers between devices  6.73 us (3%)
    all_gather x1, waiting for transfers between devices, on_device(): piece = lax.all_gather(device_total[None], 'seq', axis=0, tiled=True)  62.3 us
    dot_general x1, matrix products, on_device(): jnp.einsum('cthld,clhde->cthe', scaled, far_states, preferred_element_typ...  19.7 us
    dot_general x1, matrix products, on_device(): jnp.einsum('chtu,cuhd->cthd', prev_scores, prev_values, preferred_element...  15.8 us
    dot_general x1, matrix products, on_device(): jnp.einsum('cbj,jhde->cbhde', jnp.asarray(inner_selector(block_count, inn...  13.3 us
    dot_general x1, matrix products, on_device(): jnp.einsum('chtu,cuhd->cthd', own_scores, value_blocks, preferred_element...  12.6 us
    add x1, local copies, waits for them, and re-layouts, on_device(): weight_blocks[:, :, :, 0:1] * own_part  11.5 us
    ppermute x1, waiting for transfers between devices, shifted(): return lax.ppermute(x, axis, pairs)  10.9 us
    dot_general x1, matrix products, on_device(): jnp.einsum('ln,nhde->lhde', selector, piece, preferred_element_type=jnp.f...  10.4 us
  transfers between devices with their start and end apart: 2, of which 2 were waited for; matrix products, arithmetic and copies ran while one was open for 24% of the time, Pallas kernels for 0%

commit v1 on v0

--- a/solution.py
+++ b/solution.py
@@ -15,15 +15,6 @@
     devices = lax.axis_size(axis)
     pairs = [(i, i + by) for i in range(devices) if 0 <= i + by < devices]
     return lax.ppermute(x, axis, pairs)
-
-
-def inner_selector(block_count, inner_bits):
-    table = np.zeros((block_count, max(inner_bits - 1, 0), block_count), np.float32)
-    for target in range(block_count):
-        for source in range(target - 1):
-            highest = (target ^ source).bit_length() - 1
-            table[target, highest - 1, source] = 1.0
-    return table
 
 
 def on_device(queries, key_rows, value_rows, level_weights, out_gain):
@@ -66,23 +57,35 @@
     halo_state = jnp.einsum(
         "uhd,uhe->hde", halo_keys, halo_values, preferred_element_type=jnp.float32
     )
-    device_total = jnp.sum(block_states, 0).astype(jnp.bfloat16)
-    piece = lax.all_gather(device_total[None], "seq", axis=0, tiled=True)
-    sources = jnp.arange(piece.shape[0], dtype=jnp.int32)
-    selector_rows = []
-    for add_level_bit in range(seq_bits):
-        same_above = sources >> add_level_bit + 1 == seq_index >> add_level_bit + 1
-        source_low = sources >> add_level_bit & 1 == 0
-        target_high = seq_index >> add_level_bit & 1 == 1
-        selector_rows.append((same_above & source_low & target_high).astype(jnp.bfloat16))
-    selector = jnp.stack(selector_rows)
-    group_sums = jnp.einsum("ln,nhde->lhde", selector, piece, preferred_element_type=jnp.float32)
-    inner_states = jnp.einsum(
-        "cbj,jhde->cbhde",
-        jnp.asarray(inner_selector(block_count, inner_bits)),
-        block_states,
-        precision=lax.Precision.HIGHEST,
-    )
+    device_total = jnp.sum(block_states, 0).astype(jnp.bfloat16).astype(jnp.float32)
+    seq_count = lax.axis_size("seq")
+    group_rows = []
+    running = device_total
+    for level_bit in range(seq_bits):
+        span = 1 << level_bit
+        pairs = [(i, i ^ span) for i in range(seq_count)]
+        partner = lax.ppermute(running, "seq", pairs)
+        target_high = (seq_index >> level_bit & 1 == 1).astype(jnp.float32)
+        group_rows.append(target_high * partner)
+        if level_bit + 1 < seq_bits:
+            running = running + partner
+    group_sums = jnp.stack(group_rows)
+    inner_rows = []
+    for target in range(block_count):
+        level_rows = []
+        for level_bit in range(1, inner_bits):
+            span = 1 << level_bit
+            if target >> level_bit & 1:
+                start = target >> level_bit + 1 << level_bit + 1
+                total = block_states[start]
+                for source in range(start + 1, start + span):
+                    if source != target - 1:
+                        total = total + block_states[source]
+                level_rows.append(total)
+            else:
+                level_rows.append(jnp.zeros_like(block_states[0]))
+        if level_rows:
+            inner_rows.append(jnp.stack(level_rows))
     lowest_flags = jnp.stack(
         [
             ((seq_index >> level_bit & 1 == 1) & (seq_index & (1 << level_bit) - 1 == 0)).astype(
@@ -94,7 +97,10 @@
     first_block = (jnp.arange(block_count) == 0).astype(jnp.float32)
     correction = lowest_flags[:, None, None, None] * halo_state[None]
     outer_states = group_sums[None] - first_block[:, None, None, None, None] * correction[None]
-    far_states = jnp.concatenate([inner_states, outer_states], 1).astype(jnp.bfloat16)
+    if inner_rows:
+        inner_states = jnp.stack(inner_rows)
+        outer_states = jnp.concatenate([inner_states, outer_states], 1)
+    far_states = outer_states.astype(jnp.bfloat16)
     weight_blocks = jnp.transpose(
         level_weights.reshape(level_count, head_count, block_count, STRETCH), (2, 3, 1, 0)
     )

time: 264 us -> 269 us (1.019)
  the two profiles are of different devices: /device:TPU:0 before, /device:TPU:25 now
where the time goes in v1:
time: 269 us; the launch traced here: 267 us
  waiting for transfers between devices  102 us (38%)
  local copies, waits for them, and re-layouts  59.5 us (22%)
  matrix products  56.8 us (21%)
  other arithmetic  40.6 us (15%)
  starting transfers between devices  5.87 us (2%)
    ppermute x4, waiting for transfers between devices, on_device(): partner = lax.ppermute(running, 'seq', pairs)  102 us
    dot_general x1, matrix products, on_device(): jnp.einsum('cthld,clhde->cthe', scaled, far_states, preferred_element_typ...  19.7 us
    dot_general x1, matrix products, on_device(): jnp.einsum('chtu,cuhd->cthd', prev_scores, prev_values, preferred_element...  15.6 us
    dot_general x1, matrix products, on_device(): jnp.einsum('chtu,cuhd->cthd', own_scores, value_blocks, preferred_element...  12.5 us
    another operation x2, other arithmetic  11.8 us
    add x1, local copies, waits for them, and re-layouts, on_device(): weight_blocks[:, :, :, 0:1] * own_part  11.5 us
    another operation x5, other arithmetic, on_device(): group_sums = jnp.stack(group_rows)  10.4 us
    slice x2, local copies, waits for them, and re-layouts, on_device(): prev_values = jnp.concatenate([halo_values[None], value_blocks[:-1]], 0)  9.28 us
  transfers between devices with their start and end apart: 5, of which 4 were waited for; matrix products, arithmetic and copies ran while one was open for 22% of the time, Pallas kernels for 0%

profile of v1, /device:TPU:25, one launch (start us, length us, event | category | flops | bytes accessed | tf_op | source)
XLA Modules:
  0.0 267.1 jit_solution(5628402090538237820)
XLA Ops:
  0.0 7.5 %copy.72 = bf16[4,256,16,128]{1,3,2,0:T(8,128)(2,1)} copy(bf16[4,256,16,128]{3,2,1,0:T(8,128)(2,1)} %bitcast.69) | data formatting | bytes 8388608 | tf_op jit(solution)/shard_map/reshape | solution.py:29
  7.5 7.0 %fusion.57 = (bf16[16,128,128]{2,1,0:T(8,128)(2,1)S(1)}, f32[4,16,128,128]{3,2,1,0:T(8,128)}) fusion(bf16[4,256,16,128]{1,3,2,0:T(8,128)(2,1)} %copy.72, bf16[4,256,16,128]{3,2,1,0:T(8,128)(2,1)} %bitcast.67), kind=kOutput, calls=%fused_computation.71 | convolution fusion | flops 537657344 | bytes 13107200 | tf_op jit(solution)/shard_map/cuhd,cuhe->chde/dot_general | solution.py:54
  14.4 1.1 convert_element_type.81
  15.5 1.2 collective-permute-start.1
  16.7 1.4 slice.42
  18.1 1.4 slice.43
  19.6 0.5 copy_bitcast_fusion
  20.1 19.8 %collective-permute-done.1 = f32[16,128,128]{2,1,0:T(8,128)} collective-permute-done((f32[16,128,128]{2,1,0:T(8,128)}, f32[16,128,128]{2,1,0:T(8,128)}, u32[]{:S(2)}, u32[]{:S(2)}) %collective-permute-start.1) | collective-permute-done | bytes 1048608 | tf_op jit(solution)/shard_map/ppermute | solution.py:67
  39.9 2.8 %multiply_bitcast_fusion.3 = (f32[1,16,128,128]{3,2,1,0:T(8,128)}, f32[16,128,128]{2,1,0:T(8,128)}) fusion(f32[16,128,128]{2,1,0:T(8,128)} %collective-permute-done.1, f32[]{:T(128)} %convert_element_type.53, bf16[16,128,128]{2,1,0:T(8,128)(2,1)S(1)} %get-tuple-element.15), kind=kLoop, calls=%fused_computation.49 | loop fusion | flops 786432 | bytes 3670020 | tf_op jit(solution)/shard_map/stack | solution.py:72
  42.7 1.2 collective-permute-start.2
  43.9 1.5 pad_maximum_fusion.1
  45.4 3.1 %collective-permute-start = (bf16[2,256,16,128]{3,1,2,0:T(8,128)(2,1)}, bf16[2,256,16,128]{3,1,2,0:T(8,128)(2,1)}, u32[]{:S(2)}, u32[]{:S(2)}) collective-permute-start(bf16[2,256,16,128]{3,1,2,0:T(8,128)(2,1)} %pad_maximum_fusion.1), channel_id=1, source_target_pairs={{0,2},{2,4},{4,6},{6,8},{8,10},{10,12},{12,14},{14,16},{16,18},{18... | collective-permute-start | bytes 6291464 | tf_op jit(solution)/shard_map/ppermute | solution.py:17
  48.5 0.0 copy-start
  48.5 4.3 %slice.45 = bf16[768,16,128]{2,1,0:T(8,128)(2,1)} slice(bf16[1024,16,128]{2,1,0:T(8,128)(2,1)} %param.7), slice={[0:768], [0:16], [0:128]} | slice | bytes 6291456 | tf_op jit(solution)/shard_map/slice | solution.py:36
  52.8 0.0 copy-done
  52.8 0.5 slice.48
  53.4 2.1 fusion.42
  55.5 2.0 copy.74
  57.6 2.5 fusion.43
  60.1 2.1 copy.75
  62.1 0.0 copy-start.7
  62.1 6.6 %copy.79 = f32[4,256,16,128]{3,1,2,0:T(8,128)} copy(bf16[4,256,16,128]{3,2,1,0:T(8,128)(2,1)} %bitcast.72) | data formatting | bytes 12582912 | tf_op jit(solution)/shard_map/convert_element_type | solution.py:108
  68.7 0.0 copy-done.7
  68.8 0.0 copy-start.5
  68.8 0.8 copy-done.5
  69.6 1.0 copy.80
  70.6 5.0 %copy.68 = bf16[3,256,16,128]{1,3,2,0:T(8,128)(2,1)} copy(bf16[3,256,16,128]{3,2,1,0:T(8,128)(2,1)} %bitcast.71) | data formatting | bytes 6291456 | tf_op jit(solution)/shard_map/slice | solution.py:36
  75.6 2.5 copy.69
  78.1 0.9 slice_bitcast_fusion.1
  79.0 32.2 %collective-permute-done.2 = f32[16,128,128]{2,1,0:T(8,128)} collective-permute-done((f32[16,128,128]{2,1,0:T(8,128)}, f32[16,128,128]{2,1,0:T(8,128)}, u32[]{:S(2)}, u32[]{:S(2)}) %collective-permute-start.2) | collective-permute-done | bytes 1048608 | tf_op jit(solution)/shard_map/ppermute | solution.py:67
  111.1 1.7 multiply_bitcast_fusion.2
  112.8 0.2 collective-permute-start.3
  113.0 12.5 %fusion.27 = f32[4,16,256,128]{3,2,1,0:T(8,128)} fusion(bf16[4,256,16,128]{3,2,1,0:T(8,128)(2,1)} %bitcast.68, bf16[4,256,16,128]{1,3,2,0:T(8,128)(2,1)} %copy.72, pred[256,256]{1,0:T(8,128)(4,1)S(1)} %iota_compare_fusion, bf16[4,256,16,128]{3,2,1,0:T(8,128)(2,1)} %bitcast.73), kind=kOutput, calls=%fused_computation.33 | convolution fusion | flops 2160066560 | bytes 21037056 | tf_op jit(solution)/shard_map/chtu,cuhd->cthd/dot_general | solution.py:48
  125.6 9.7 %collective-permute-done.3 = f32[16,128,128]{2,1,0:T(8,128)} collective-permute-done((f32[16,128,128]{2,1,0:T(8,128)S(1)}, f32[16,128,128]{2,1,0:T(8,128)}, u32[]{:S(2)}, u32[]{:S(2)}) %collective-permute-start.3) | collective-permute-done | bytes 1048608 | tf_op jit(solution)/shard_map/ppermute | solution.py:67
  135.3 2.4 multiply_bitcast_fusion.1
  137.7 0.1 collective-permute-start.4
  137.7 0.1 pad_maximum_fusion.2
  137.8 0.0 collective-permute-done
  137.8 2.7 %fusion.56 = (bf16[1,256,16,128]{3,1,2,0:T(8,128)(2,1)S(1)}, bf16[1,256,16,128]{3,1,2,0:T(8,128)(2,1)}) fusion(bf16[2,256,16,128]{3,1,2,0:T(8,128)(2,1)} %collective-permute-done), kind=kLoop, calls=%fused_computation.70 | loop fusion | bytes 4194304 | tf_op jit(solution)/shard_map/slice | solution.py:34
  140.5 1.3 copy.67
  141.8 2.0 fusion.39
  143.9 0.0 copy-start.1
  143.9 2.6 broadcast_multiply_fusion
  146.5 39.9 %collective-permute-done.4 = f32[16,128,128]{2,1,0:T(8,128)} collective-permute-done((f32[16,128,128]{2,1,0:T(8,128)}, f32[16,128,128]{2,1,0:T(8,128)}, u32[]{:S(2)}, u32[]{:S(2)}) %collective-permute-start.4) | collective-permute-done | bytes 1048608 | tf_op jit(solution)/shard_map/ppermute | solution.py:67
  186.3 1.3 multiply_bitcast_fusion
  187.7 0.0 copy-done.1
  187.7 2.2 pad_maximum_fusion
  189.9 5.4 %copy.76 = f32[4,16,128,128]{2,3,0,1:T(8,128)} copy(f32[4,16,128,128]{3,2,1,0:T(8,128)} %pad_maximum_fusion) | data formatting | bytes 8388608 | tf_op jit(solution)/shard_map/stack | solution.py:72
  195.3 0.0 copy-start.4
  195.3 9.3 %subtract_convert_fusion = bf16[4,4,16,128,128]{3,4,1,2,0:T(8,128)(2,1)} fusion(f32[4,16,128,128]{2,3,0,1:T(8,128)} %broadcast_multiply_fusion, f32[4]{0:T(128)S(1)} %compare_convert_fusion, f32[4,16,128,128]{2,3,0,1:T(8,128)} %copy.76), kind=kLoop, calls=%fused_computation.5 | loop fusion | flops 12582912 | bytes 16777232 | tf_op jit(solution)/shard_map/convert.4
  204.6 0.0 copy-done.3
  204.6 0.0 copy-done.4
  204.6 0.0 copy-start.6
  204.6 6.7 %fusion.67 = bf16[4,5,16,128,128]{3,4,1,2,0:T(8,128)(2,1)S(1)} fusion(bf16[4,4,16,128,128]{3,4,1,2,0:T(8,128)(2,1)} %subtract_convert_fusion, bf16[1,1,16,128,128]{3,4,1,2,0:T(8,128)(2,1)S(1)} %copy-done.4, bf16[1,1,16,128,128]{3,4,1,2,0:T(8,128)(2,1)S(1)} %copy-done.3, bf16[4,5]{1,0:T(4,128)(2,1)S(1)} %pad.clone), kind=kLoop, calls=%fused_computation.8.clone.2 | loop fusion | flops 15728640 | bytes 19922984 | tf_op jit(solution)/shard_map/cthld,clhde->cthe/dot_general | solution.py:110
  211.3 0.0 copy-done.6
  211.4 0.0 copy-start.2
  211.4 19.7 %fusion = f32[4,16,128,256,1]{2,3,4,1,0:T(8,128)} fusion(f32[4,256,16,5]{1,3,2,0:T(8,128)S(1)} %copy-done.6, f32[4,256,16,128]{3,1,2,0:T(8,128)} %copy.79, bf16[4,5,16,128,128]{3,4,1,2,0:T(8,128)(2,1)S(1)} %fusion.67), kind=kOutput, calls=%fused_computation.1 | convolution fusion | flops 2715811840 | bytes 27590656 | tf_op jit(solution)/shard_map/cthld,clhde->cthe/dot_general | solution.py:110
  231.1 0.0 copy-done.2
  231.1 15.6 %multiply_reduce_fusion = (f32[4,256]{1,0:T(4,128)S(1)}, f32[4,256,16,128]{3,1,2,0:T(8,128)}) fusion(f32[4,16,128,256,1]{2,3,4,1,0:T(8,128)} %fusion, bf16[3,256,16,128]{3,1,2,0:T(8,128)(2,1)} %copy.69, bf16[1,256,16,128]{3,1,2,0:T(8,128)(2,1)} %get-tuple-element.6, bf16[4,256,16,128]{3,2,1,0:T(8,128)(2,1)} %bitcast.74, ...), kind=kOutput, calls=%fused_computation.21 | convolution fusion | flops 2172648448 | bytes 37883904 | tf_op jit(solution)/shard_map/chtu,cuhd->cthd/dot_general | solution.py:51
  246.6 0.0 copy-start.8
  246.6 11.5 %copy.82 = f32[4,256,16,128]{3,2,1,0:T(8,128)} copy(f32[4,256,16,128]{3,1,2,0:T(8,128)} %get-tuple-element.18) | data formatting | bytes 16777216 | tf_op jit(solution)/shard_map/add | solution.py:114
  258.1 2.6 psum.7
  260.7 0.0 copy-done.8
  260.7 6.4 %fusion.11 = bf16[1024,16,128]{2,1,0:T(8,128)(2,1)} fusion(f32[4,256,16,128]{3,2,1,0:T(8,128)} %copy.82, f32[16,128]{1,0:T(8,128)S(1)} %copy-done.8, f32[1024]{0:T(1024)S(1)} %add_rsqrt_fusion), kind=kLoop, calls=%fused_computation.17 | loop fusion | flops 6291456 | bytes 12595200 | tf_op jit(solution)/shard_map/convert_element_type | solution.py:120
  (9 shorter events, 0.1 us)
Async XLA Ops:
  15.5 24.4 %collective-permute-start.1 = (f32[16,128,128]{2,1,0:T(8,128)}, f32[16,128,128]{2,1,0:T(8,128)}, u32[]{:S(2)}, u32[]{:S(2)}) collective-permute-start(f32[16,128,128]{2,1,0:T(8,128)} %convert_element_type.81), channel_id=1, source_target_pairs={{0,2},{2,0},{4,6},{6,4},{8,10},{10,8},{12,14},{14,12},{16,18},{18,... | collective-permute-start | bytes 3145736 | tf_op jit(solution)/shard_map/ppermute | solution.py:67
  42.7 68.4 %collective-permute-start.2 = (f32[16,128,128]{2,1,0:T(8,128)}, f32[16,128,128]{2,1,0:T(8,128)}, u32[]{:S(2)}, u32[]{:S(2)}) collective-permute-start(f32[16,128,128]{2,1,0:T(8,128)} %get-tuple-element.8), channel_id=1, source_target_pairs={{0,4},{2,6},{4,0},{6,2},{8,12},{10,14},{12,8},{14,10},{16,20},{18,... | collective-permute-start | bytes 3145736 | tf_op jit(solution)/shard_map/ppermute | solution.py:67
  45.4 92.4 %collective-permute-start = (bf16[2,256,16,128]{3,1,2,0:T(8,128)(2,1)}, bf16[2,256,16,128]{3,1,2,0:T(8,128)(2,1)}, u32[]{:S(2)}, u32[]{:S(2)}) collective-permute-start(bf16[2,256,16,128]{3,1,2,0:T(8,128)(2,1)} %pad_maximum_fusion.1), channel_id=1, source_target_pairs={{0,2},{2,4},{4,6},{6,8},{8,10},{10,12},{12,14},{14,16},{16,18},{18... | collective-permute-start | bytes 6291464 | tf_op jit(solution)/shard_map/ppermute | solution.py:17
  48.5 4.3 %copy-start = (bf16[1024,16,128]{2,1,0:T(8,128)(2,1)S(1)}, bf16[1024,16,128]{2,1,0:T(8,128)(2,1)}, u32[]{:S(2)}) copy-start(bf16[1024,16,128]{2,1,0:T(8,128)(2,1)} %param.6) | copy-start | bytes 12582916
  62.1 6.6 %copy-start.7 = (f32[7,16,1024]{2,1,0:T(8,128)S(1)}, f32[7,16,1024]{2,1,0:T(8,128)}, u32[]{:S(2)}) copy-start(f32[7,16,1024]{2,1,0:T(8,128)} %param.8) | copy-start | bytes 1376260
  68.8 0.8 copy-start.5
  112.8 22.5 %collective-permute-start.3 = (f32[16,128,128]{2,1,0:T(8,128)S(1)}, f32[16,128,128]{2,1,0:T(8,128)}, u32[]{:S(2)}, u32[]{:S(2)}) collective-permute-start(f32[16,128,128]{2,1,0:T(8,128)S(1)} %get-tuple-element.10), channel_id=1, source_target_pairs={{0,8},{2,10},{4,12},{6,14},{8,0},{10,2},{12,4},{14,6},{16,24},{18,... | collective-permute-start | bytes 3145736 | tf_op jit(solution)/shard_map/ppermute | solution.py:67
  137.7 48.7 %collective-permute-start.4 = (f32[16,128,128]{2,1,0:T(8,128)}, f32[16,128,128]{2,1,0:T(8,128)}, u32[]{:S(2)}, u32[]{:S(2)}) collective-permute-start(f32[16,128,128]{2,1,0:T(8,128)} %get-tuple-element.12), channel_id=1, source_target_pairs={{0,16},{2,18},{4,20},{6,22},{8,24},{10,26},{12,28},{14,30},{16,0},... | collective-permute-start | bytes 3145736 | tf_op jit(solution)/shard_map/ppermute | solution.py:67
  143.9 43.8 %copy-start.1 = (f32[1,16,128,128]{3,2,1,0:T(8,128)S(1)}, f32[1,16,128,128]{3,2,1,0:T(8,128)}, u32[]{:S(2)}) copy-start(f32[1,16,128,128]{3,2,1,0:T(8,128)} %get-tuple-element.7) | copy-start | bytes 3145732
  195.3 9.3 %copy-start.3 = (bf16[1,1,16,128,128]{3,4,1,2,0:T(8,128)(2,1)S(1)}, bf16[1,1,16,128,128]{3,4,1,2,0:T(8,128)(2,1)}, u32[]{:S(2)}) copy-start(bf16[1,1,16,128,128]{3,4,1,2,0:T(8,128)(2,1)} %copy.74) | copy-start | bytes 1572868
  195.3 9.3 %copy-start.4 = (bf16[1,1,16,128,128]{3,4,1,2,0:T(8,128)(2,1)S(1)}, bf16[1,1,16,128,128]{3,4,1,2,0:T(8,128)(2,1)}, u32[]{:S(2)}) copy-start(bf16[1,1,16,128,128]{3,4,1,2,0:T(8,128)(2,1)} %copy.75) | copy-start | bytes 1572868
  204.6 6.7 %copy-start.6 = (f32[4,256,16,5]{1,3,2,0:T(8,128)S(1)}, f32[4,256,16,5]{1,3,2,0:T(8,128)}, u32[]{:S(2)}) copy-start(f32[4,256,16,5]{1,3,2,0:T(8,128)} %copy.80) | copy-start | bytes 983044
  211.4 19.7 %copy-start.2 = (bf16[3,256,16,128]{1,3,2,0:T(8,128)(2,1)S(1)}, bf16[3,256,16,128]{1,3,2,0:T(8,128)(2,1)}, u32[]{:S(2)}) copy-start(bf16[3,256,16,128]{1,3,2,0:T(8,128)(2,1)} %copy.68) | copy-start | bytes 9437188
  246.6 14.1 %copy-start.8 = (f32[16,128]{1,0:T(8,128)S(1)}, f32[16,128]{1,0:T(8,128)}, u32[]{:S(2)}) copy-start(f32[16,128]{1,0:T(8,128)} %param.9) | copy-start | bytes 24580

commit v2 on v1

--- a/solution.py
+++ b/solution.py
@@ -64,7 +64,9 @@
     for level_bit in range(seq_bits):
         span = 1 << level_bit
         pairs = [(i, i ^ span) for i in range(seq_count)]
-        partner = lax.ppermute(running, "seq", pairs)
+        if level_bit + 1 == seq_bits:
+            pairs = [(i, i ^ span) for i in range(seq_count) if not i & span]
+        partner = lax.ppermute(running.astype(jnp.bfloat16), "seq", pairs).astype(jnp.float32)
         target_high = (seq_index >> level_bit & 1 == 1).astype(jnp.float32)
         group_rows.append(target_high * partner)
         if level_bit + 1 < seq_bits:

time: 269 us -> 228 us (0.85)
  the two profiles are of different devices: /device:TPU:25 before, /device:TPU:0 now
where the time goes in v2:
time: 228 us; the launch traced here: 227 us
  local copies, waits for them, and re-layouts  59.9 us (26%)
  waiting for transfers between devices  57.6 us (25%)
  matrix products  56.8 us (25%)
  other arithmetic  34 us (15%)
  starting transfers between devices  16.5 us (7%)
  blocking collectives  2.44 us (1%)
    ppermute x4, waiting for transfers between devices, on_device(): lax.ppermute(running.astype(jnp.bfloat16), 'seq', pairs).astype(jnp.float32)  57.6 us
    dot_general x1, matrix products, on_device(): jnp.einsum('cthld,clhde->cthe', scaled, far_states, preferred_element_typ...  19.7 us
    dot_general x1, matrix products, on_device(): jnp.einsum('chtu,cuhd->cthd', prev_scores, prev_values, preferred_element...  15.6 us
    dot_general x1, matrix products, on_device(): jnp.einsum('chtu,cuhd->cthd', own_scores, value_blocks, preferred_element...  12.5 us
    ppermute x4, starting transfers between devices, on_device(): lax.ppermute(running.astype(jnp.bfloat16), 'seq', pairs).astype(jnp.float32)  11.8 us
    add x1, local copies, waits for them, and re-layouts, on_device(): weight_blocks[:, :, :, 0:1] * own_part  11.5 us
    another operation x2, other arithmetic  10.3 us
    reshape x1, local copies, waits for them, and re-layouts, on_device(): key_blocks = key_rows.reshape(block_count, STRETCH, head_count, head_width)  7.45 us
  transfers between devices with their start and end apart: 5, of which 2 were waited for; matrix products, arithmetic and copies ran while one was open for 25% of the time, Pallas kernels for 0%

profile of v2, /device:TPU:0, one launch (start us, length us, event | category | flops | bytes accessed | tf_op | source)
XLA Modules:
  0.0 227.4 jit_solution(2695677164308384250)
XLA Ops:
  0.0 7.5 %copy.72 = bf16[4,256,16,128]{1,3,2,0:T(8,128)(2,1)} copy(bf16[4,256,16,128]{3,2,1,0:T(8,128)(2,1)} %bitcast.71) | data formatting | bytes 8388608 | tf_op jit(solution)/shard_map/reshape | solution.py:29
  7.5 7.0 %fusion.62 = (bf16[16,128,128]{2,1,0:T(8,128)(2,1)S(1)}, f32[4,16,128,128]{3,2,1,0:T(8,128)}) fusion(bf16[4,256,16,128]{1,3,2,0:T(8,128)(2,1)} %copy.72, bf16[4,256,16,128]{3,2,1,0:T(8,128)(2,1)} %bitcast.69), kind=kOutput, calls=%fused_computation.78 | convolution fusion | flops 537657344 | bytes 13107200 | tf_op jit(solution)/shard_map/cuhd,cuhe->chde/dot_general | solution.py:54
  14.4 3.0 %collective-permute-start.1 = (bf16[16,128,128]{2,1,0:T(8,128)(2,1)S(1)}, bf16[16,128,128]{2,1,0:T(8,128)(2,1)S(1)}, u32[]{:S(2)}, u32[]{:S(2)}) collective-permute-start(bf16[16,128,128]{2,1,0:T(8,128)(2,1)S(1)} %get-tuple-element.13), channel_id=1, source_target_pairs={{0,2},{2,0},{4,6},{6,4},{8,10},{10,8},{12,14},{14,12},{16,18},{18,... | collective-permute-start | bytes 1572872 | tf_op jit(solution)/shard_map/ppermute | solution.py:69
  17.5 11.9 %collective-permute-done.1 = bf16[16,128,128]{2,1,0:T(8,128)(2,1)S(1)} collective-permute-done((bf16[16,128,128]{2,1,0:T(8,128)(2,1)S(1)}, bf16[16,128,128]{2,1,0:T(8,128)(2,1)S(1)}, u32[]{:S(2)}, u32[]{:S(2)}) %collective-permute-start.1) | collective-permute-done | bytes 524320 | tf_op jit(solution)/shard_map/ppermute | solution.py:69
  29.4 0.1 fusion.46
  29.6 1.8 collective-permute-start.2
  31.4 1.4 slice.43
  32.8 1.4 slice.42
  34.2 0.3 copy.112
  34.5 0.3 copy.113
  34.8 1.5 pad_maximum_fusion.1
  36.3 4.7 %collective-permute-start = (bf16[2,256,16,128]{3,1,2,0:T(8,128)(2,1)}, bf16[2,256,16,128]{3,1,2,0:T(8,128)(2,1)}, u32[]{:S(2)}, u32[]{:S(2)}) collective-permute-start(bf16[2,256,16,128]{3,1,2,0:T(8,128)(2,1)} %pad_maximum_fusion.1), channel_id=1, source_target_pairs={{0,2},{2,4},{4,6},{6,8},{8,10},{10,12},{12,14},{14,16},{16,18},{18... | collective-permute-start | bytes 6291464 | tf_op jit(solution)/shard_map/ppermute | solution.py:17
  41.0 45.7 %collective-permute-done.2 = bf16[16,128,128]{2,1,0:T(8,128)(2,1)S(1)} collective-permute-done((bf16[16,128,128]{2,1,0:T(8,128)(2,1)S(1)}, bf16[16,128,128]{2,1,0:T(8,128)(2,1)S(1)}, u32[]{:S(2)}, u32[]{:S(2)}) %collective-permute-start.2) | collective-permute-done | bytes 524320 | tf_op jit(solution)/shard_map/ppermute | solution.py:69
  86.7 0.2 fusion.47
  86.9 1.6 collective-permute-start.3
  88.5 12.5 %fusion.27 = f32[4,16,256,128]{3,2,1,0:T(8,128)} fusion(bf16[4,256,16,128]{3,2,1,0:T(8,128)(2,1)} %bitcast.70, bf16[4,256,16,128]{1,3,2,0:T(8,128)(2,1)} %copy.72, pred[256,256]{1,0:T(8,128)(4,1)S(1)} %iota_compare_fusion, bf16[4,256,16,128]{3,2,1,0:T(8,128)(2,1)} %bitcast.74), kind=kOutput, calls=%fused_computation.33 | convolution fusion | flops 2160066560 | bytes 21037056 | tf_op jit(solution)/shard_map/chtu,cuhd->cthd/dot_general | solution.py:48
  101.1 0.0 copy-start.1
  101.1 2.3 %fusion.48 = bf16[1,1,16,128,128]{4,3,2,1,0:T(8,128)(2,1)} fusion(f32[4,16,128,128]{3,2,1,0:T(8,128)} %get-tuple-element.14), kind=kLoop, calls=%fused_computation.60 | loop fusion | bytes 1048576 | tf_op jit(solution)/shard_map/convert.6
  103.4 0.0 collective-permute-done.3
  103.4 2.5 %fusion.38 = (f32[1,16,128,128]{3,2,1,0:T(8,128)}, bf16[16,128,128]{2,1,0:T(8,128)(2,1)}, f32[1,16,128,128]{3,2,1,0:T(8,128)}, f32[1,16,128,128]{3,2,1,0:T(8,128)}) fusion(bf16[16,128,128]{2,1,0:T(8,128)(2,1)S(1)} %collective-permute-done.1, f32[]{:T(128)} %convert_element_type.75, bf16[16,128,128]{2,1,0:T(8,128)(2,1)S(1)} %collective-permute-done.3, ...), kind=kLoop, calls=%fused_computation.45 | loop fusion | flops 2883584 | bytes 5767180 | tf_op jit(solution)/shard_map/stack | solution.py:74
  105.9 5.3 %collective-permute-start.4 = (bf16[16,128,128]{2,1,0:T(8,128)(2,1)}, bf16[16,128,128]{2,1,0:T(8,128)(2,1)}, u32[]{:S(2)}, u32[]{:S(2)}) collective-permute-start(bf16[16,128,128]{2,1,0:T(8,128)(2,1)} %get-tuple-element.8), channel_id=1, source_target_pairs={{0,16},{2,18},{4,20},{6,22},{8,24},{10,26},{12,28},{14,30},{1,17},... | collective-permute-start | bytes 1572872 | tf_op jit(solution)/shard_map/ppermute | solution.py:69
  111.1 0.0 copy-done.1
  111.1 0.9 fusion.49
  112.0 0.0 copy-start
  112.1 6.7 %copy.79 = f32[4,256,16,128]{3,1,2,0:T(8,128)} copy(bf16[4,256,16,128]{3,2,1,0:T(8,128)(2,1)} %bitcast.75) | data formatting | bytes 12582912 | tf_op jit(solution)/shard_map/convert_element_type | solution.py:110
  118.7 0.0 copy-done
  118.7 2.2 slice.45
  120.9 1.1 copy-done.2
  122.0 0.5 slice.48
  122.6 2.0 copy.74
  124.7 2.1 copy.75
  126.7 1.1 copy.114
  127.8 0.0 copy-start.9
  127.8 0.8 copy-done.9
  128.6 1.0 copy.80
  129.6 5.0 %copy.68 = bf16[3,256,16,128]{1,3,2,0:T(8,128)(2,1)} copy(bf16[3,256,16,128]{3,2,1,0:T(8,128)(2,1)} %bitcast.73) | data formatting | bytes 6291456 | tf_op jit(solution)/shard_map/slice | solution.py:36
  134.6 2.5 %copy.69 = bf16[3,256,16,128]{3,1,2,0:T(8,128)(2,1)} copy(bf16[3,256,16,128]{3,2,1,0:T(8,128)(2,1)S(1)} %bitcast.72) | data formatting | bytes 6291456 | tf_op jit(solution)/shard_map/slice | solution.py:35
  137.1 0.1 pad_maximum_fusion.2
  137.1 0.9 slice_bitcast_fusion.1
  138.0 0.0 collective-permute-done.4
  138.0 1.1 multiply_bitcast_fusion
  139.2 0.0 copy-done.3
  139.2 0.0 copy-done.4
  139.2 0.0 copy-done.5
  139.2 2.4 %pad_maximum_fusion = f32[4,16,128,128]{3,2,1,0:T(8,128)} fusion(f32[1,16,128,128]{3,2,1,0:T(8,128)S(1)} %multiply_bitcast_fusion, f32[1,16,128,128]{3,2,1,0:T(8,128)S(1)} %copy-done.5, f32[1,16,128,128]{3,2,1,0:T(8,128)S(1)} %copy-done.4, f32[1,16,128,128]{3,2,1,0:T(8,128)S(1)} %copy-done.3), kind=kLoop, calls=%fused_computation.30 | loop fusion | flops 3145728 | bytes 8388608 | tf_op jit(solution)/shard_map/stack | solution.py:74
  141.7 5.4 %copy.76 = f32[4,16,128,128]{2,3,0,1:T(8,128)} copy(f32[4,16,128,128]{3,2,1,0:T(8,128)} %pad_maximum_fusion) | data formatting | bytes 8388608 | tf_op jit(solution)/shard_map/stack | solution.py:74
  147.1 0.0 collective-permute-done
  147.1 2.7 %fusion.61 = (bf16[1,256,16,128]{3,1,2,0:T(8,128)(2,1)S(1)}, bf16[1,256,16,128]{3,1,2,0:T(8,128)(2,1)}) fusion(bf16[2,256,16,128]{3,1,2,0:T(8,128)(2,1)} %collective-permute-done), kind=kLoop, calls=%fused_computation.77 | loop fusion | bytes 4194304 | tf_op jit(solution)/shard_map/slice | solution.py:34
  149.8 1.3 copy.67
  151.1 2.0 fusion.43
  153.1 2.6 %broadcast_multiply_fusion = f32[4,16,128,128]{2,3,0,1:T(8,128)} fusion(f32[16,128,128]{1,2,0:T(8,128)S(1)} %fusion.43, f32[4]{0:T(128)S(1)} %pad_maximum_fusion.2), kind=kLoop, calls=%fused_computation.38 | loop fusion | flops 1048576 | bytes 5242896 | tf_op jit(solution)/shard_map/mul | solution.py:100
  155.7 9.3 %subtract_convert_fusion = bf16[4,4,16,128,128]{3,4,1,2,0:T(8,128)(2,1)} fusion(f32[4,16,128,128]{2,3,0,1:T(8,128)} %broadcast_multiply_fusion, f32[4]{0:T(128)S(1)} %compare_convert_fusion, f32[4,16,128,128]{2,3,0,1:T(8,128)} %copy.76), kind=kLoop, calls=%fused_computation.5 | loop fusion | flops 12582912 | bytes 16777232 | tf_op jit(solution)/shard_map/convert.4
  165.0 0.0 copy-done.7
  165.0 0.0 copy-done.8
  165.0 6.7 %fusion.72 = bf16[4,5,16,128,128]{3,4,1,2,0:T(8,128)(2,1)S(1)} fusion(bf16[4,4,16,128,128]{3,4,1,2,0:T(8,128)(2,1)} %subtract_convert_fusion, bf16[1,1,16,128,128]{3,4,1,2,0:T(8,128)(2,1)S(1)} %copy-done.8, bf16[1,1,16,128,128]{3,4,1,2,0:T(8,128)(2,1)S(1)} %copy-done.7, bf16[4,5]{1,0:T(4,128)(2,1)S(1)} %pad.clone), kind=kLoop, calls=%fused_computation.8.clone.2 | loop fusion | flops 15728640 | bytes 19922984 | tf_op jit(solution)/shard_map/cthld,clhde->cthe/dot_general | solution.py:112
  171.8 0.0 copy-done.10
  171.8 0.0 copy-start.6
  171.8 19.7 %fusion = f32[4,16,128,256,1]{2,3,4,1,0:T(8,128)} fusion(f32[4,256,16,5]{1,3,2,0:T(8,128)S(1)} %copy-done.10, f32[4,256,16,128]{3,1,2,0:T(8,128)} %copy.79, bf16[4,5,16,128,128]{3,4,1,2,0:T(8,128)(2,1)S(1)} %fusion.72), kind=kOutput, calls=%fused_computation.1 | convolution fusion | flops 2715811840 | bytes 27590656 | tf_op jit(solution)/shard_map/cthld,clhde->cthe/dot_general | solution.py:112
  191.5 0.0 copy-done.6
  191.5 15.6 %multiply_reduce_fusion = (f32[4,256]{1,0:T(4,128)S(1)}, f32[4,256,16,128]{3,1,2,0:T(8,128)}) fusion(f32[4,16,128,256,1]{2,3,4,1,0:T(8,128)} %fusion, bf16[3,256,16,128]{3,1,2,0:T(8,128)(2,1)} %copy.69, bf16[1,256,16,128]{3,1,2,0:T(8,128)(2,1)} %get-tuple-element.6, bf16[4,256,16,128]{3,2,1,0:T(8,128)(2,1)} %bitcast.76, ...), kind=kOutput, calls=%fused_computation.21 | convolution fusion | flops 2172648448 | bytes 37883904 | tf_op jit(solution)/shard_map/chtu,cuhd->cthd/dot_general | solution.py:51
  207.1 11.5 %copy.82 = f32[4,256,16,128]{3,2,1,0:T(8,128)} copy(f32[4,256,16,128]{3,1,2,0:T(8,128)} %get-tuple-element.16) | data formatting | bytes 16777216 | tf_op jit(solution)/shard_map/add | solution.py:116
  218.6 2.4 %psum.7 = f32[1024]{0:T(1024)S(1)} all-reduce(f32[1024]{0:T(1024)S(1)} %bitcast.82), channel_id=1, replica_groups=mesh['seq'=16,'head'=2] {'head'}, use_global_device_ids=true, to_apply=%region_2.3 | all-reduce | flops 1024 | bytes 8192 | tf_op jit(solution)/shard_map/psum | solution.py:120
  221.0 0.0 copy-done.11
  221.0 6.4 %fusion.11 = bf16[1024,16,128]{2,1,0:T(8,128)(2,1)} fusion(f32[4,256,16,128]{3,2,1,0:T(8,128)} %copy.82, f32[16,128]{1,0:T(8,128)S(1)} %copy-done.11, f32[1024]{0:T(1024)S(1)} %add_rsqrt_fusion), kind=kLoop, calls=%fused_computation.17 | loop fusion | flops 6291456 | bytes 12595200 | tf_op jit(solution)/shard_map/convert_element_type | solution.py:122
  (15 shorter events, 0.1 us)
Async XLA Ops:
  14.4 15.0 %collective-permute-start.1 = (bf16[16,128,128]{2,1,0:T(8,128)(2,1)S(1)}, bf16[16,128,128]{2,1,0:T(8,128)(2,1)S(1)}, u32[]{:S(2)}, u32[]{:S(2)}) collective-permute-start(bf16[16,128,128]{2,1,0:T(8,128)(2,1)S(1)} %get-tuple-element.13), channel_id=1, source_target_pairs={{0,2},{2,0},{4,6},{6,4},{8,10},{10,8},{12,14},{14,12},{16,18},{18,... | collective-permute-start | bytes 1572872 | tf_op jit(solution)/shard_map/ppermute | solution.py:69
  29.6 57.1 %collective-permute-start.2 = (bf16[16,128,128]{2,1,0:T(8,128)(2,1)S(1)}, bf16[16,128,128]{2,1,0:T(8,128)(2,1)S(1)}, u32[]{:S(2)}, u32[]{:S(2)}) collective-permute-start(bf16[16,128,128]{2,1,0:T(8,128)(2,1)S(1)} %fusion.46), channel_id=1, source_target_pairs={{0,4},{2,6},{4,0},{6,2},{8,12},{10,14},{12,8},{14,10},{16,20},{18,... | collective-permute-start | bytes 1572872 | tf_op jit(solution)/shard_map/ppermute | solution.py:69
  36.3 110.8 %collective-permute-start = (bf16[2,256,16,128]{3,1,2,0:T(8,128)(2,1)}, bf16[2,256,16,128]{3,1,2,0:T(8,128)(2,1)}, u32[]{:S(2)}, u32[]{:S(2)}) collective-permute-start(bf16[2,256,16,128]{3,1,2,0:T(8,128)(2,1)} %pad_maximum_fusion.1), channel_id=1, source_target_pairs={{0,2},{2,4},{4,6},{6,8},{8,10},{10,12},{12,14},{14,16},{16,18},{18... | collective-permute-start | bytes 6291464 | tf_op jit(solution)/shard_map/ppermute | solution.py:17
  86.9 16.5 %collective-permute-start.3 = (bf16[16,128,128]{2,1,0:T(8,128)(2,1)S(1)}, bf16[16,128,128]{2,1,0:T(8,128)(2,1)S(1)}, u32[]{:S(2)}, u32[]{:S(2)}) collective-permute-start(bf16[16,128,128]{2,1,0:T(8,128)(2,1)S(1)} %fusion.47), channel_id=1, source_target_pairs={{0,8},{2,10},{4,12},{6,14},{8,0},{10,2},{12,4},{14,6},{16,24},{18,... | collective-permute-start | bytes 1572872 | tf_op jit(solution)/shard_map/ppermute | solution.py:69
  101.1 10.1 %copy-start.1 = (f32[4,16,128,128]{3,2,1,0:T(8,128)S(1)}, f32[4,16,128,128]{3,2,1,0:T(8,128)}, u32[]{:S(2)}) copy-start(f32[4,16,128,128]{3,2,1,0:T(8,128)} %get-tuple-element.14) | copy-start | bytes 12582916
  105.9 32.2 %collective-permute-start.4 = (bf16[16,128,128]{2,1,0:T(8,128)(2,1)}, bf16[16,128,128]{2,1,0:T(8,128)(2,1)}, u32[]{:S(2)}, u32[]{:S(2)}) collective-permute-start(bf16[16,128,128]{2,1,0:T(8,128)(2,1)} %get-tuple-element.8), channel_id=1, source_target_pairs={{0,16},{2,18},{4,20},{6,22},{8,24},{10,26},{12,28},{14,30},{1,17},... | collective-permute-start | bytes 1572872 | tf_op jit(solution)/shard_map/ppermute | solution.py:69
  112.0 6.7 %copy-start = (bf16[1024,16,128]{2,1,0:T(8,128)(2,1)S(1)}, bf16[1024,16,128]{2,1,0:T(8,128)(2,1)}, u32[]{:S(2)}) copy-start(bf16[1024,16,128]{2,1,0:T(8,128)(2,1)} %param.7) | copy-start | bytes 12582916
  118.7 3.3 %copy-start.2 = (bf16[1024,16,128]{2,1,0:T(8,128)(2,1)S(1)}, bf16[1024,16,128]{2,1,0:T(8,128)(2,1)}, u32[]{:S(2)}) copy-start(bf16[1024,16,128]{2,1,0:T(8,128)(2,1)} %param.6) | copy-start | bytes 12582916
  127.8 0.8 copy-start.9
  134.6 4.6 %copy-start.3 = (f32[1,16,128,128]{3,2,1,0:T(8,128)S(1)}, f32[1,16,128,128]{3,2,1,0:T(8,128)}, u32[]{:S(2)}) copy-start(f32[1,16,128,128]{3,2,1,0:T(8,128)} %get-tuple-element.7) | copy-start | bytes 3145732
  134.6 4.6 %copy-start.4 = (f32[1,16,128,128]{3,2,1,0:T(8,128)S(1)}, f32[1,16,128,128]{3,2,1,0:T(8,128)}, u32[]{:S(2)}) copy-start(f32[1,16,128,128]{3,2,1,0:T(8,128)} %get-tuple-element.9) | copy-start | bytes 3145732
  134.6 4.6 %copy-start.5 = (f32[1,16,128,128]{3,2,1,0:T(8,128)S(1)}, f32[1,16,128,128]{3,2,1,0:T(8,128)}, u32[]{:S(2)}) copy-start(f32[1,16,128,128]{3,2,1,0:T(8,128)} %get-tuple-element.10) | copy-start | bytes 3145732
  155.7 9.3 %copy-start.7 = (bf16[1,1,16,128,128]{3,4,1,2,0:T(8,128)(2,1)S(1)}, bf16[1,1,16,128,128]{3,4,1,2,0:T(8,128)(2,1)}, u32[]{:S(2)}) copy-start(bf16[1,1,16,128,128]{3,4,1,2,0:T(8,128)(2,1)} %copy.74) | copy-start | bytes 1572868
  155.7 9.3 %copy-start.8 = (bf16[1,1,16,128,128]{3,4,1,2,0:T(8,128)(2,1)S(1)}, bf16[1,1,16,128,128]{3,4,1,2,0:T(8,128)(2,1)}, u32[]{:S(2)}) copy-start(bf16[1,1,16,128,128]{3,4,1,2,0:T(8,128)(2,1)} %copy.75) | copy-start | bytes 1572868
  165.0 6.7 %copy-start.10 = (f32[4,256,16,5]{1,3,2,0:T(8,128)S(1)}, f32[4,256,16,5]{1,3,2,0:T(8,128)}, u32[]{:S(2)}) copy-start(f32[4,256,16,5]{1,3,2,0:T(8,128)} %copy.80) | copy-start | bytes 983044
  171.8 19.7 %copy-start.6 = (bf16[3,256,16,128]{1,3,2,0:T(8,128)(2,1)S(1)}, bf16[3,256,16,128]{1,3,2,0:T(8,128)(2,1)}, u32[]{:S(2)}) copy-start(bf16[3,256,16,128]{1,3,2,0:T(8,128)(2,1)} %copy.68) | copy-start | bytes 9437188
  207.1 13.9 %copy-start.11 = (f32[16,128]{1,0:T(8,128)S(1)}, f32[16,128]{1,0:T(8,128)}, u32[]{:S(2)}) copy-start(f32[16,128]{1,0:T(8,128)} %param.9) | copy-start | bytes 24580

commit v3 on v2

--- a/solution.py
+++ b/solution.py
@@ -67,6 +67,8 @@
         if level_bit + 1 == seq_bits:
             pairs = [(i, i ^ span) for i in range(seq_count) if not i & span]
         partner = lax.ppermute(running.astype(jnp.bfloat16), "seq", pairs).astype(jnp.float32)
+        if level_bit == min(1, seq_bits - 1):
+            partner, own_part, prev_part = lax.optimization_barrier((partner, own_part, prev_part))
         target_high = (seq_index >> level_bit & 1 == 1).astype(jnp.float32)
         group_rows.append(target_high * partner)
         if level_bit + 1 < seq_bits:

time: 228 us -> 213 us (0.934)
  the two profiles are of different devices: /device:TPU:0 before, /device:TPU:25 now
where the time goes in v3:
time: 213 us; the launch traced here: 212 us
  matrix products  55.1 us (26%)
  starting transfers between devices  51.2 us (24%)
  local copies, waits for them, and re-layouts  42.9 us (20%)
  other arithmetic  33.6 us (16%)
  waiting for transfers between devices  25.5 us (12%)
  blocking collectives  3.64 us (2%)
    ppermute x4, starting transfers between devices, on_device(): lax.ppermute(running.astype(jnp.bfloat16), 'seq', pairs).astype(jnp.float32)  49 us
    ppermute x4, waiting for transfers between devices, on_device(): lax.ppermute(running.astype(jnp.bfloat16), 'seq', pairs).astype(jnp.float32)  25.5 us
    dot_general x1, matrix products, on_device(): jnp.einsum('cthld,clhde->cthe', scaled, far_states, preferred_element_typ...  23.2 us
    dot_general x1, matrix products, on_device(): jnp.einsum('chtu,cuhd->cthd', own_scores, value_blocks, preferred_element...  12.7 us
    another operation x2, other arithmetic  10.9 us
    dot_general x1, matrix products, on_device(): jnp.einsum('chtu,cuhd->cthd', prev_scores, prev_values, preferred_element...  9.58 us
    add x1, local copies, waits for them, and re-layouts, on_device(): weight_blocks[:, :, :, 0:1] * own_part  8.25 us
    dot_general x1, matrix products, on_device(): jnp.einsum('cuhd,cuhe->chde', key_blocks, value_blocks, preferred_element...  7.57 us
  transfers between devices with their start and end apart: 5, of which 2 were waited for; matrix products, arithmetic and copies ran while one was open for 22% of the time, Pallas kernels for 0%

profile of v3, /device:TPU:25, one launch (start us, length us, event | category | flops | bytes accessed | tf_op | source)
XLA Modules:
  0.0 212.1 jit_solution(6724309486213884604)
XLA Ops:
  0.0 7.6 %fusion.71 = (bf16[16,128,128]{2,1,0:T(8,128)(2,1)S(1)}, f32[4,16,128,128]{3,2,1,0:T(8,128)}) fusion(bf16[4,256,16,128]{3,2,1,0:T(8,128)(2,1)} %bitcast.61, bf16[4,256,16,128]{3,2,1,0:T(8,128)(2,1)} %bitcast.59), kind=kOutput, calls=%fused_computation.78 | convolution fusion | flops 537657344 | bytes 13107200 | tf_op jit(solution)/shard_map/cuhd,cuhe->chde/dot_general | solution.py:54
  7.6 0.0 copy-start.1
  7.6 1.3 collective-permute-start
  8.9 1.4 slice.41
  10.3 1.4 slice.42
  11.7 0.5 copy_bitcast_fusion
  12.2 1.5 pad_maximum_fusion.1
  13.8 2.2 %collective-permute-start.2 = (bf16[2,256,16,128]{3,1,2,0:T(8,128)(2,1)}, bf16[2,256,16,128]{3,1,2,0:T(8,128)(2,1)}, u32[]{:S(2)}, u32[]{:S(2)}) collective-permute-start(bf16[2,256,16,128]{3,1,2,0:T(8,128)(2,1)} %pad_maximum_fusion.1), channel_id=1, source_target_pairs={{0,2},{2,4},{4,6},{6,8},{8,10},{10,12},{12,14},{14,16},{16,18},{18... | collective-permute-start | bytes 6291464 | tf_op jit(solution)/shard_map/ppermute | solution.py:17
  15.9 4.5 %collective-permute-done = bf16[16,128,128]{2,1,0:T(8,128)(2,1)S(1)} collective-permute-done((bf16[16,128,128]{2,1,0:T(8,128)(2,1)S(1)}, bf16[16,128,128]{2,1,0:T(8,128)(2,1)S(1)}, u32[]{:S(2)}, u32[]{:S(2)}) %collective-permute-start) | collective-permute-done | bytes 524320 | tf_op jit(solution)/shard_map/ppermute | solution.py:69
  20.5 0.0 copy-done.1
  20.5 0.0 copy-start.3
  20.5 1.0 fusion.51
  21.4 0.0 copy-done.3
  21.4 46.3 %collective-permute-start.1 = (bf16[16,128,128]{2,1,0:T(8,128)(2,1)}, bf16[16,128,128]{2,1,0:T(8,128)(2,1)}, u32[]{:S(2)}, u32[]{:S(2)}) collective-permute-start(bf16[16,128,128]{2,1,0:T(8,128)(2,1)} %fusion.51), channel_id=1, source_target_pairs={{0,4},{2,6},{4,0},{6,2},{8,12},{10,14},{12,8},{14,10},{16,20},{18,... | collective-permute-start | bytes 1572872 | tf_op jit(solution)/shard_map/ppermute | solution.py:69
  67.7 12.7 %fusion.33 = f32[4,256,16,128]{3,1,2,0:T(8,128)} fusion(bf16[4,256,16,128]{3,2,1,0:T(8,128)(2,1)} %bitcast.62, pred[256,256]{1,0:T(8,128)(4,1)S(1)} %iota_compare_fusion, bf16[4,256,16,128]{3,2,1,0:T(8,128)(2,1)} %bitcast.60, bf16[4,256,16,128]{3,2,1,0:T(8,128)(2,1)} %bitcast.65), kind=kOutput, calls=%fused_computation.36 | convolution fusion | flops 2160066560 | bytes 21037056 | tf_op jit(solution)/shard_map/chtu,cuhd->cthd/dot_general | solution.py:48
  80.5 0.0 copy-start
  80.5 2.6 %slice.47 = bf16[768,16,128]{2,1,0:T(8,128)(2,1)S(1)} slice(bf16[1024,16,128]{2,1,0:T(8,128)(2,1)} %param.6), slice={[0:768], [0:16], [0:128]} | slice | bytes 6291456 | tf_op jit(solution)/shard_map/slice | solution.py:35
  83.0 0.6 copy-done
  83.6 0.5 slice.44
  84.1 2.4 %copy.71 = bf16[3,256,16,128]{3,1,2,0:T(8,128)(2,1)} copy(bf16[3,256,16,128]{3,2,1,0:T(8,128)(2,1)S(1)} %bitcast.64) | data formatting | bytes 6291456 | tf_op jit(solution)/shard_map/slice | solution.py:35
  86.6 3.5 %copy.70 = bf16[3,256,16,128]{1,3,2,0:T(8,128)(2,1)} copy(bf16[3,256,16,128]{3,2,1,0:T(8,128)(2,1)S(1)} %bitcast.63) | data formatting | bytes 6291456 | tf_op jit(solution)/shard_map/slice | solution.py:36
  90.1 2.1 %fusion.56 = bf16[1,1,16,128,128]{4,3,2,1,0:T(8,128)(2,1)} fusion(f32[4,16,128,128]{3,2,1,0:T(8,128)} %get-tuple-element.20), kind=kLoop, calls=%fused_computation.59 | loop fusion | bytes 1048576 | tf_op jit(solution)/shard_map/convert.6
  92.2 0.0 collective-permute-done.1
  92.2 1.1 convert_element_type.77
  93.4 0.0 collective-permute-done.2
  93.4 2.7 %fusion.70 = (bf16[1,256,16,128]{3,1,2,0:T(8,128)(2,1)S(1)}, bf16[1,256,16,128]{3,1,2,0:T(8,128)(2,1)}) fusion(bf16[2,256,16,128]{3,1,2,0:T(8,128)(2,1)} %collective-permute-done.2), kind=kLoop, calls=%fused_computation.77 | loop fusion | bytes 4194304 | tf_op jit(solution)/shard_map/slice | solution.py:34
  96.1 0.5 copy.69
  96.6 0.0 copy-start.2
  96.6 0.0 copy-start.4
  96.6 9.6 %fusion.36 = f32[4,256,16,128]{3,1,2,0:T(8,128)} fusion(bf16[3,256,16,128]{3,1,2,0:T(8,128)(2,1)} %copy.71, bf16[1,256,16,128]{3,1,2,0:T(8,128)(2,1)} %get-tuple-element.12, bf16[4,256,16,128]{3,2,1,0:T(8,128)(2,1)} %bitcast.66, bf16[3,256,16,128]{1,3,2,0:T(8,128)(2,1)} %copy.70, bf16[1,256,16,128]{1,3,2,0:T(8,128)(2,1)S(1)} %copy.69), kind=kOutput, calls=%fused_computation.37 | convolution fusion | flops 2160066560 | bytes 20971520 | tf_op jit(solution)/shard_map/chtu,cuhd->cthd/dot_general | solution.py:51
  106.2 0.0 copy-done.2
  106.2 0.0 copy-done.4
  106.2 1.0 fusion.58
  107.2 0.2 collective-permute-start.3
  107.4 1.7 fusion.57
  109.1 0.0 copy-start.7
  109.1 6.6 %copy.79 = f32[4,256,16,128]{3,1,2,0:T(8,128)} copy(bf16[4,256,16,128]{3,2,1,0:T(8,128)(2,1)} %bitcast.67) | data formatting | bytes 12582912 | tf_op jit(solution)/shard_map/convert_element_type | solution.py:112
  115.6 0.0 copy-done.7
  115.7 0.0 copy-start.5
  115.7 0.7 copy-done.5
  116.4 1.0 copy.80
  117.5 0.3 copy.75
  117.7 1.3 copy.74
  119.1 0.1 pad_maximum_fusion.2
  119.2 0.9 slice_bitcast_fusion.1
  120.1 0.0 collective-permute-done.3
  120.1 1.6 multiply_bitcast_fusion.1
  121.7 1.3 collective-permute-start.4
  123.0 2.0 fusion.47
  125.0 2.6 %broadcast_multiply_fusion = f32[4,16,128,128]{2,3,0,1:T(8,128)} fusion(f32[16,128,128]{1,2,0:T(8,128)S(1)} %fusion.47, f32[4]{0:T(128)S(1)} %pad_maximum_fusion.2), kind=kLoop, calls=%fused_computation.39 | loop fusion | flops 1048576 | bytes 5242896 | tf_op jit(solution)/shard_map/mul | solution.py:102
  127.6 20.9 %collective-permute-done.4 = bf16[16,128,128]{2,1,0:T(8,128)(2,1)S(1)} collective-permute-done((bf16[16,128,128]{2,1,0:T(8,128)(2,1)S(1)}, bf16[16,128,128]{2,1,0:T(8,128)(2,1)S(1)}, u32[]{:S(2)}, u32[]{:S(2)}) %collective-permute-start.4) | collective-permute-done | bytes 524320 | tf_op jit(solution)/shard_map/ppermute | solution.py:69
  148.5 0.1 multiply_bitcast_fusion
  148.6 2.2 %pad_maximum_fusion = f32[4,16,128,128]{3,2,1,0:T(8,128)} fusion(f32[1,16,128,128]{3,2,1,0:T(8,128)S(1)} %multiply_bitcast_fusion, f32[1,16,128,128]{3,2,1,0:T(8,128)S(1)} %get-tuple-element.16, f32[1,16,128,128]{3,2,1,0:T(8,128)S(1)} %get-tuple-element.13, f32[1,16,128,128]{3,2,1,0:T(8,128)S(1)} %get-tuple-element.15), kind=kLoop, calls=%fused_computation.27 | loop fusion | flops 3145728 | bytes 8388608 | tf_op jit(solution)/shard_map/stack | solution.py:76
  150.9 5.4 %copy.76 = f32[4,16,128,128]{2,3,0,1:T(8,128)} copy(f32[4,16,128,128]{3,2,1,0:T(8,128)} %pad_maximum_fusion) | data formatting | bytes 8388608 | tf_op jit(solution)/shard_map/stack | solution.py:76
  156.3 9.3 %subtract_convert_fusion = bf16[4,4,16,128,128]{3,4,1,2,0:T(8,128)(2,1)} fusion(f32[4,16,128,128]{2,3,0,1:T(8,128)} %broadcast_multiply_fusion, f32[4]{0:T(128)S(1)} %compare_convert_fusion, f32[4,16,128,128]{2,3,0,1:T(8,128)} %copy.76), kind=kLoop, calls=%fused_computation.5 | loop fusion | flops 12582912 | bytes 16777232 | tf_op jit(solution)/shard_map/convert.4
  165.5 0.0 copy-start.6
  165.5 6.7 %fusion.63.clone.5 = bf16[4,5,16,128,128]{3,4,1,2,0:T(8,128)(2,1)S(1)} fusion(bf16[4,4,16,128,128]{3,4,1,2,0:T(8,128)(2,1)} %subtract_convert_fusion, bf16[1,1,16,128,128]{3,4,1,2,0:T(8,128)(2,1)S(1)} %copy.75, bf16[1,1,16,128,128]{3,4,1,2,0:T(8,128)(2,1)S(1)} %copy.74, bf16[4,5]{1,0:T(4,128)(2,1)S(1)} %pad.clone), kind=kLoop, calls=%fused_computation.8.clone.clone.clone.clone.clone.2 | loop fusion | flops 15728640 | bytes 19922984 | tf_op jit(solution)/shard_map/reduce_sum | solution.py:121
  172.2 0.0 copy-done.6
  172.2 23.2 %multiply_reduce_fusion = (f32[4,256]{1,0:T(4,128)S(1)}, f32[4,256,16,128]{3,1,2,0:T(8,128)}) fusion(f32[4,256,16,5]{1,3,2,0:T(8,128)S(1)} %copy-done.6, f32[4,256,16,128]{3,1,2,0:T(8,128)} %copy.79, f32[4,256,16,128]{3,1,2,0:T(8,128)} %fusion.36, f32[4,256,16]{1,2,0:T(8,128)S(1)} %get-tuple-element.18, f32[4,256,16,128]{3,1,2,0:T(8,128)} %fusion.33, ...), kind=kOutput, calls=%fused_computation.18 | convolution fusion | flops 2728393728 | bytes 44503040 | tf_op jit(solution)/shard_map/cthld,clhde->cthe/dot_general | solution.py:114
  195.5 3.6 %psum.7 = f32[1024]{0:T(1024)S(1)} all-reduce(f32[1024]{0:T(1024)S(1)} %bitcast.71), channel_id=1, replica_groups=mesh['seq'=16,'head'=2] {'head'}, use_global_device_ids=true, to_apply=%region_2.3 | all-reduce | flops 1024 | bytes 8192 | tf_op jit(solution)/shard_map/psum | solution.py:122
  199.1 0.0 copy-start.8
  199.1 8.3 %copy.82 = f32[4,256,16,128]{3,2,1,0:T(8,128)S(1)} copy(f32[4,256,16,128]{3,1,2,0:T(8,128)} %get-tuple-element.22) | data formatting | bytes 16777216 | tf_op jit(solution)/shard_map/add | solution.py:118
  207.4 0.0 copy-done.8
  207.4 4.7 %fusion.11 = bf16[1024,16,128]{2,1,0:T(8,128)(2,1)} fusion(f32[4,256,16,128]{3,2,1,0:T(8,128)S(1)} %copy.82, f32[16,128]{1,0:T(8,128)S(1)} %copy-done.8, f32[1024]{0:T(1024)S(1)} %add_rsqrt_fusion), kind=kLoop, calls=%fused_computation.17 | loop fusion | flops 6291456 | bytes 12595200 | tf_op jit(solution)/shard_map/convert_element_type | solution.py:124
  (8 shorter events, 0.1 us)
Async XLA Ops:
  7.6 12.9 %copy-start.1 = (bf16[16,128,128]{2,1,0:T(8,128)(2,1)}, bf16[16,128,128]{2,1,0:T(8,128)(2,1)S(1)}, u32[]{:S(2)}) copy-start(bf16[16,128,128]{2,1,0:T(8,128)(2,1)S(1)} %get-tuple-element.19) | copy-start | bytes 1572868
  7.6 12.9 %collective-permute-start = (bf16[16,128,128]{2,1,0:T(8,128)(2,1)S(1)}, bf16[16,128,128]{2,1,0:T(8,128)(2,1)S(1)}, u32[]{:S(2)}, u32[]{:S(2)}) collective-permute-start(bf16[16,128,128]{2,1,0:T(8,128)(2,1)S(1)} %get-tuple-element.19), channel_id=1, source_target_pairs={{0,2},{2,0},{4,6},{6,4},{8,10},{10,8},{12,14},{14,12},{16,18},{18,... | collective-permute-start | bytes 1572872 | tf_op jit(solution)/shard_map/ppermute | solution.py:69
  13.8 79.6 %collective-permute-start.2 = (bf16[2,256,16,128]{3,1,2,0:T(8,128)(2,1)}, bf16[2,256,16,128]{3,1,2,0:T(8,128)(2,1)}, u32[]{:S(2)}, u32[]{:S(2)}) collective-permute-start(bf16[2,256,16,128]{3,1,2,0:T(8,128)(2,1)} %pad_maximum_fusion.1), channel_id=1, source_target_pairs={{0,2},{2,4},{4,6},{6,8},{8,10},{10,12},{12,14},{14,16},{16,18},{18... | collective-permute-start | bytes 6291464 | tf_op jit(solution)/shard_map/ppermute | solution.py:17
  20.5 1.0 copy-start.3
  21.4 70.8 %collective-permute-start.1 = (bf16[16,128,128]{2,1,0:T(8,128)(2,1)}, bf16[16,128,128]{2,1,0:T(8,128)(2,1)}, u32[]{:S(2)}, u32[]{:S(2)}) collective-permute-start(bf16[16,128,128]{2,1,0:T(8,128)(2,1)} %fusion.51), channel_id=1, source_target_pairs={{0,4},{2,6},{4,0},{6,2},{8,12},{10,14},{12,8},{14,10},{16,20},{18,... | collective-permute-start | bytes 1572872 | tf_op jit(solution)/shard_map/ppermute | solution.py:69
  80.5 3.1 %copy-start = (bf16[1024,16,128]{2,1,0:T(8,128)(2,1)S(1)}, bf16[1024,16,128]{2,1,0:T(8,128)(2,1)}, u32[]{:S(2)}) copy-start(bf16[1024,16,128]{2,1,0:T(8,128)(2,1)} %param.7) | copy-start | bytes 12582916
  96.6 9.6 %copy-start.2 = (bf16[16,128,128]{2,1,0:T(8,128)(2,1)S(1)}, bf16[16,128,128]{2,1,0:T(8,128)(2,1)}, u32[]{:S(2)}) copy-start(bf16[16,128,128]{2,1,0:T(8,128)(2,1)} %copy-done.1) | copy-start | bytes 1572868
  96.6 9.6 %copy-start.4 = (bf16[16,128,128]{2,1,0:T(8,128)(2,1)S(1)}, bf16[16,128,128]{2,1,0:T(8,128)(2,1)}, u32[]{:S(2)}) copy-start(bf16[16,128,128]{2,1,0:T(8,128)(2,1)} %copy-done.3) | copy-start | bytes 1572868
  107.2 12.9 %collective-permute-start.3 = (bf16[16,128,128]{2,1,0:T(8,128)(2,1)}, bf16[16,128,128]{2,1,0:T(8,128)(2,1)}, u32[]{:S(2)}, u32[]{:S(2)}) collective-permute-start(bf16[16,128,128]{2,1,0:T(8,128)(2,1)} %fusion.58), channel_id=1, source_target_pairs={{0,8},{2,10},{4,12},{6,14},{8,0},{10,2},{12,4},{14,6},{16,24},{18,... | collective-permute-start | bytes 1572872 | tf_op jit(solution)/shard_map/ppermute | solution.py:69
  109.1 6.6 %copy-start.7 = (f32[7,16,1024]{2,1,0:T(8,128)S(1)}, f32[7,16,1024]{2,1,0:T(8,128)}, u32[]{:S(2)}) copy-start(f32[7,16,1024]{2,1,0:T(8,128)} %param.8) | copy-start | bytes 1376260
  115.7 0.8 copy-start.5
  121.7 26.9 %collective-permute-start.4 = (bf16[16,128,128]{2,1,0:T(8,128)(2,1)S(1)}, bf16[16,128,128]{2,1,0:T(8,128)(2,1)S(1)}, u32[]{:S(2)}, u32[]{:S(2)}) collective-permute-start(bf16[16,128,128]{2,1,0:T(8,128)(2,1)S(1)} %get-tuple-element.14), channel_id=1, source_target_pairs={{0,16},{2,18},{4,20},{6,22},{8,24},{10,26},{12,28},{14,30},{1,17},... | collective-permute-start | bytes 1572872 | tf_op jit(solution)/shard_map/ppermute | solution.py:69
  165.5 6.7 %copy-start.6 = (f32[4,256,16,5]{1,3,2,0:T(8,128)S(1)}, f32[4,256,16,5]{1,3,2,0:T(8,128)}, u32[]{:S(2)}) copy-start(f32[4,256,16,5]{1,3,2,0:T(8,128)} %copy.80) | copy-start | bytes 983044
  199.1 8.3 %copy-start.8 = (f32[16,128]{1,0:T(8,128)S(1)}, f32[16,128]{1,0:T(8,128)}, u32[]{:S(2)}) copy-start(f32[16,128]{1,0:T(8,128)} %param.9) | copy-start | bytes 24580

commit v4 on v3

--- a/solution.py
+++ b/solution.py
@@ -57,6 +57,12 @@
     halo_state = jnp.einsum(
         "uhd,uhe->hde", halo_keys, halo_values, preferred_element_type=jnp.float32
     )
+    weight_blocks = jnp.transpose(
+        level_weights.reshape(level_count, head_count, block_count, STRETCH), (2, 3, 1, 0)
+    )
+    scaled = (
+        query_blocks[:, :, :, None, :] * weight_blocks[:, :, :, 2:, None] * score_scale
+    ).astype(jnp.bfloat16)
     device_total = jnp.sum(block_states, 0).astype(jnp.bfloat16).astype(jnp.float32)
     seq_count = lax.axis_size("seq")
     group_rows = []
@@ -68,7 +74,9 @@
             pairs = [(i, i ^ span) for i in range(seq_count) if not i & span]
         partner = lax.ppermute(running.astype(jnp.bfloat16), "seq", pairs).astype(jnp.float32)
         if level_bit == min(1, seq_bits - 1):
-            partner, own_part, prev_part = lax.optimization_barrier((partner, own_part, prev_part))
+            partner, own_part, prev_part, scaled = lax.optimization_barrier(
+                (partner, own_part, prev_part, scaled)
+            )
         target_high = (seq_index >> level_bit & 1 == 1).astype(jnp.float32)
         group_rows.append(target_high * partner)
         if level_bit + 1 < seq_bits:
@@ -105,12 +113,6 @@
         inner_states = jnp.stack(inner_rows)
         outer_states = jnp.concatenate([inner_states, outer_states], 1)
     far_states = outer_states.astype(jnp.bfloat16)
-    weight_blocks = jnp.transpose(
-        level_weights.reshape(level_count, head_count, block_count, STRETCH), (2, 3, 1, 0)
-    )
-    scaled = (
-        query_blocks[:, :, :, None, :] * weight_blocks[:, :, :, 2:, None] * score_scale
-    ).astype(jnp.bfloat16)
     far_part = jnp.einsum(
         "cthld,clhde->cthe", scaled, far_states, preferred_element_type=jnp.float32
     )

time: 213 us -> 203 us (0.953)
  starting transfers between devices: 51.2 us -> 8.27 us
  waiting for transfers between devices: 25.5 us -> 66.5 us
  local copies, waits for them, and re-layouts: 42.9 us -> 35.5 us
  other arithmetic: 33.6 us -> 40.2 us
  matrix products: 55.1 us -> 48.7 us
    ppermute x4, starting transfers between devices: 49 us -> 4.9 us  [on_device(): lax.ppermute(running.astype(jnp.bfloat16), 'seq', pairs).astype(jnp.float32)]
    ppermute x4, waiting for transfers between devices: 25.5 us -> 66.5 us  [on_device(): lax.ppermute(running.astype(jnp.bfloat16), 'seq', pairs).astype(jnp.float32)]
    convert_element_type x0 -> x1, other arithmetic: none -> 13.3 us  [on_device(): scaled = (query_blocks[:, :, :, None, :] * weight_blocks[:, :, :, 2:, Non...]
    reduce_sum x1 -> x0, other arithmetic: 6.69 us -> none  [on_device(): square_sum = jnp.sum(mixed_out * mixed_out, axis=(1, 2))]
    dot_general x1, matrix products: 7.57 us -> 4.11 us  [on_device(): jnp.einsum('cuhd,cuhe->chde', key_blocks, value_blocks, preferred_element...]
    dot_general x1, matrix products: 23.2 us -> 19.9 us  [on_device(): jnp.einsum('cthld,clhde->cthe', scaled, far_states, preferred_element_typ...]
    convert_element_type x1, local copies, waits for them, and re-layouts: 6.56 us -> 3.33 us  [on_device(): query_blocks[:, :, :, None, :] * weight_blocks[:, :, :, 2:, None]]
  transfers between devices with their start and end apart: 5 -> 5, of which waited for: 2 -> 3; matrix products, arithmetic and copies ran while one was open for 22% -> 26% of each run, Pallas kernels for 0% -> 0%
where the time goes in v4:
time: 203 us; the launch traced here: 202 us
  waiting for transfers between devices  66.5 us (33%)
  matrix products  48.7 us (24%)
  other arithmetic  40.2 us (20%)
  local copies, waits for them, and re-layouts  35.5 us (17%)
  starting transfers between devices  8.27 us (4%)
  blocking collectives  2.6 us (1%)
    ppermute x4, waiting for transfers between devices, on_device(): lax.ppermute(running.astype(jnp.bfloat16), 'seq', pairs).astype(jnp.float32)  66.5 us
    dot_general x1, matrix products, on_device(): jnp.einsum('cthld,clhde->cthe', scaled, far_states, preferred_element_typ...  19.9 us
    convert_element_type x1, other arithmetic, on_device(): scaled = (query_blocks[:, :, :, None, :] * weight_blocks[:, :, :, 2:, Non...  13.3 us
    dot_general x1, matrix products, on_device(): jnp.einsum('chtu,cuhd->cthd', own_scores, value_blocks, preferred_element...  12.8 us
    another operation x2, other arithmetic  10.9 us
    dot_general x1, matrix products, on_device(): jnp.einsum('chtu,cuhd->cthd', prev_scores, prev_values, preferred_element...  9.89 us
    add x1, local copies, waits for them, and re-layouts, on_device(): weight_blocks[:, :, :, 0:1] * own_part  8.25 us
    another operation x1, local copies, waits for them, and re-layouts, on_device(): group_sums = jnp.stack(group_rows)  5.39 us
  transfers between devices with their start and end apart: 5, of which 3 were waited for; matrix products, arithmetic and copies ran while one was open for 26% of the time, Pallas kernels for 0%

profile of v4, /device:TPU:25, one launch (start us, length us, event | category | flops | bytes accessed | tf_op | source)
XLA Modules:
  0.0 202.0 jit_solution(2956050235422266532)
XLA Ops:
  0.0 0.0 slice-start
  0.0 0.0 slice-start.1
  0.0 1.2 slice-done
  1.2 0.3 slice-done.1
  1.5 0.0 copy-start
  1.5 0.0 copy-start.2
  1.5 0.5 copy_bitcast_fusion
  2.1 1.5 pad_maximum_fusion.1
  3.6 3.4 %collective-permute-start.2 = (bf16[2,256,16,128]{3,1,2,0:T(8,128)(2,1)}, bf16[2,256,16,128]{3,1,2,0:T(8,128)(2,1)}, u32[]{:S(2)}, u32[]{:S(2)}) collective-permute-start(bf16[2,256,16,128]{3,1,2,0:T(8,128)(2,1)} %pad_maximum_fusion.1), channel_id=1, source_target_pairs={{0,2},{2,4},{4,6},{6,8},{8,10},{10,12},{12,14},{14,16},{16,18},{18... | collective-permute-start | bytes 6291464 | tf_op jit(solution)/shard_map/ppermute | solution.py:17
  7.0 0.0 copy-done
  7.0 0.0 copy-done.2
  7.0 4.1 %fusion.67 = (bf16[16,128,128]{2,1,0:T(8,128)(2,1)S(1)}, f32[4,16,128,128]{3,2,1,0:T(8,128)}) fusion(bf16[4,256,16,128]{3,2,1,0:T(8,128)(2,1)S(1)} %bitcast.62, bf16[4,256,16,128]{3,2,1,0:T(8,128)(2,1)S(1)} %bitcast.60), kind=kOutput, calls=%fused_computation.74 | convolution fusion | flops 537657344 | bytes 13107200 | tf_op jit(solution)/shard_map/cuhd,cuhe->chde/dot_general | solution.py:54
  11.1 0.0 copy-start.4
  11.1 1.3 collective-permute-start
  12.4 12.8 %fusion.32 = f32[4,256,16,128]{3,1,2,0:T(8,128)} fusion(bf16[4,256,16,128]{3,2,1,0:T(8,128)(2,1)} %bitcast.61, pred[256,256]{1,0:T(8,128)(4,1)S(1)} %iota_compare_fusion, bf16[4,256,16,128]{3,2,1,0:T(8,128)(2,1)} %bitcast.59, bf16[4,256,16,128]{3,2,1,0:T(8,128)(2,1)} %bitcast.65), kind=kOutput, calls=%fused_computation.33 | convolution fusion | flops 2160066560 | bytes 21037056 | tf_op jit(solution)/shard_map/chtu,cuhd->cthd/dot_general | solution.py:48
  25.2 3.3 %copy.74 = f32[4,256,16,128]{3,1,2,0:T(8,128)S(1)} copy(bf16[4,256,16,128]{3,2,1,0:T(8,128)(2,1)} %bitcast.66) | data formatting | bytes 12582912 | tf_op jit(solution)/shard_map/convert_element_type | solution.py:64
  28.6 0.0 copy-done.10
  28.6 0.0 copy-start.8
  28.7 0.2 copy.75
  28.9 35.8 %collective-permute-done = bf16[16,128,128]{2,1,0:T(8,128)(2,1)S(1)} collective-permute-done((bf16[16,128,128]{2,1,0:T(8,128)(2,1)S(1)}, bf16[16,128,128]{2,1,0:T(8,128)(2,1)S(1)}, u32[]{:S(2)}, u32[]{:S(2)}) %collective-permute-start) | collective-permute-done | bytes 524320 | tf_op jit(solution)/shard_map/ppermute | solution.py:75
  64.7 0.0 copy-done.4
  64.7 0.0 copy-done.8
  64.7 1.0 fusion.50
  65.7 2.2 %collective-permute-start.1 = (bf16[16,128,128]{2,1,0:T(8,128)(2,1)}, bf16[16,128,128]{2,1,0:T(8,128)(2,1)}, u32[]{:S(2)}, u32[]{:S(2)}) collective-permute-start(bf16[16,128,128]{2,1,0:T(8,128)(2,1)} %fusion.50), channel_id=1, source_target_pairs={{0,4},{2,6},{4,0},{6,2},{8,12},{10,14},{12,8},{14,10},{16,20},{18,... | collective-permute-start | bytes 1572872 | tf_op jit(solution)/shard_map/ppermute | solution.py:75
  67.8 13.3 %multiply_convert_fusion = bf16[4,256,16,5,128]{4,1,3,2,0:T(8,128)(2,1)} fusion(f32[4,256,16,5]{1,3,2,0:T(8,128)S(1)} %copy.75, f32[4,256,16,128]{3,1,2,0:T(8,128)S(1)} %copy.74), kind=kLoop, calls=%fused_computation | loop fusion | flops 31457280 | bytes 29687808 | tf_op jit(solution)/shard_map/convert_element_type | solution.py:65
  81.1 0.0 copy-done.6
  81.1 0.0 copy-done.1
  81.1 0.5 slice.47
  81.6 1.6 copy-done.3
  83.3 0.5 slice.44
  83.8 2.4 %copy.71 = bf16[3,256,16,128]{3,1,2,0:T(8,128)(2,1)} copy(bf16[3,256,16,128]{3,2,1,0:T(8,128)(2,1)S(1)} %bitcast.64) | data formatting | bytes 6291456 | tf_op jit(solution)/shard_map/slice | solution.py:35
  86.2 3.4 %copy.70 = bf16[3,256,16,128]{1,3,2,0:T(8,128)(2,1)} copy(bf16[3,256,16,128]{3,2,1,0:T(8,128)(2,1)S(1)} %bitcast.63) | data formatting | bytes 6291456 | tf_op jit(solution)/shard_map/slice | solution.py:36
  89.7 1.3 fusion.55
  91.0 0.0 collective-permute-done.1
  91.0 1.1 convert_element_type.77
  92.2 0.0 collective-permute-done.2
  92.2 2.7 %fusion.66 = (bf16[1,256,16,128]{3,1,2,0:T(8,128)(2,1)S(1)}, bf16[1,256,16,128]{3,1,2,0:T(8,128)(2,1)}) fusion(bf16[2,256,16,128]{3,1,2,0:T(8,128)(2,1)} %collective-permute-done.2), kind=kLoop, calls=%fused_computation.73 | loop fusion | bytes 4194304 | tf_op jit(solution)/shard_map/slice | solution.py:34
  94.9 1.3 copy.69
  96.2 9.9 %fusion.35 = f32[4,256,16,128]{3,1,2,0:T(8,128)} fusion(bf16[3,256,16,128]{3,1,2,0:T(8,128)(2,1)} %copy.71, bf16[1,256,16,128]{3,1,2,0:T(8,128)(2,1)} %get-tuple-element.14, bf16[4,256,16,128]{3,2,1,0:T(8,128)(2,1)} %bitcast.67, bf16[3,256,16,128]{1,3,2,0:T(8,128)(2,1)} %copy.70, bf16[1,256,16,128]{1,3,2,0:T(8,128)(2,1)} %copy.69), kind=kOutput, calls=%fused_computation.34 | convolution fusion | flops 2160066560 | bytes 20971520 | tf_op jit(solution)/shard_map/chtu,cuhd->cthd/dot_general | solution.py:51
  106.1 0.0 copy-done.5
  106.1 0.0 copy-done.7
  106.1 1.0 fusion.57
  107.1 0.2 collective-permute-start.3
  107.3 1.7 fusion.56
  109.0 1.0 copy.77
  110.0 0.3 copy.76
  110.3 0.1 pad_maximum_fusion.2
  110.4 0.9 slice_bitcast_fusion.1
  111.2 8.9 %collective-permute-done.3 = bf16[16,128,128]{2,1,0:T(8,128)(2,1)} collective-permute-done((bf16[16,128,128]{2,1,0:T(8,128)(2,1)}, bf16[16,128,128]{2,1,0:T(8,128)(2,1)}, u32[]{:S(2)}, u32[]{:S(2)}) %collective-permute-start.3) | collective-permute-done | bytes 524320 | tf_op jit(solution)/shard_map/ppermute | solution.py:75
  120.1 1.6 multiply_bitcast_fusion.1
  121.7 1.3 collective-permute-start.4
  123.0 2.0 %fusion.46 = f32[16,128,128]{1,2,0:T(8,128)S(1)} fusion(bf16[2,256,16,128]{3,1,2,0:T(8,128)(2,1)} %collective-permute-done.2), kind=kOutput, calls=%fused_computation.48 | convolution fusion | flops 134217728 | bytes 3145728 | tf_op jit(solution)/shard_map/uhd,uhe->hde/dot_general | solution.py:57
  125.0 2.6 %broadcast_multiply_fusion = f32[4,16,128,128]{2,3,0,1:T(8,128)} fusion(f32[16,128,128]{1,2,0:T(8,128)S(1)} %fusion.46, f32[4]{0:T(128)S(1)} %pad_maximum_fusion.2), kind=kLoop, calls=%fused_computation.36 | loop fusion | flops 1048576 | bytes 5242896 | tf_op jit(solution)/shard_map/mul | solution.py:110
  127.6 21.8 %collective-permute-done.4 = bf16[16,128,128]{2,1,0:T(8,128)(2,1)S(1)} collective-permute-done((bf16[16,128,128]{2,1,0:T(8,128)(2,1)S(1)}, bf16[16,128,128]{2,1,0:T(8,128)(2,1)S(1)}, u32[]{:S(2)}, u32[]{:S(2)}) %collective-permute-start.4) | collective-permute-done | bytes 524320 | tf_op jit(solution)/shard_map/ppermute | solution.py:75
  149.5 0.1 multiply_bitcast_fusion
  149.6 2.2 %pad_maximum_fusion = f32[4,16,128,128]{3,2,1,0:T(8,128)} fusion(f32[1,16,128,128]{3,2,1,0:T(8,128)S(1)} %multiply_bitcast_fusion, f32[1,16,128,128]{3,2,1,0:T(8,128)S(1)} %get-tuple-element.18, f32[1,16,128,128]{3,2,1,0:T(8,128)S(1)} %get-tuple-element.15, f32[1,16,128,128]{3,2,1,0:T(8,128)S(1)} %get-tuple-element.17), kind=kLoop, calls=%fused_computation.24 | loop fusion | flops 3145728 | bytes 8388608 | tf_op jit(solution)/shard_map/stack | solution.py:84
  151.8 5.4 %copy.78 = f32[4,16,128,128]{2,3,0,1:T(8,128)} copy(f32[4,16,128,128]{3,2,1,0:T(8,128)} %pad_maximum_fusion) | data formatting | bytes 8388608 | tf_op jit(solution)/shard_map/stack | solution.py:84
  157.2 9.3 %subtract_convert_fusion = bf16[4,4,16,128,128]{3,4,1,2,0:T(8,128)(2,1)} fusion(f32[4,16,128,128]{2,3,0,1:T(8,128)} %broadcast_multiply_fusion, f32[4]{0:T(128)S(1)} %compare_convert_fusion, f32[4,16,128,128]{2,3,0,1:T(8,128)} %copy.78), kind=kLoop, calls=%fused_computation.1 | loop fusion | flops 12582912 | bytes 16777232 | tf_op jit(solution)/shard_map/convert.4
  166.5 0.0 copy-done.9
  166.5 19.9 %multiply_reduce_fusion = (f32[4,256]{1,0:T(4,128)S(1)}, f32[4,256,16,128]{3,1,2,0:T(8,128)}) fusion(bf16[4,256,16,5,128]{4,1,3,2,0:T(8,128)(2,1)} %multiply_convert_fusion, bf16[4,4,16,128,128]{3,4,1,2,0:T(8,128)(2,1)} %subtract_convert_fusion, bf16[1,1,16,128,128]{3,4,1,2,0:T(8,128)(2,1)S(1)} %copy-done.9, bf16[1,1,16,128,128]{3,4,1,2,0:T(8,128)(2,1)S(1)} %copy.76, ...), kind=kOutput, calls=%fused_computation.15 | convolution fusion | flops 2712665088 | bytes 55709736 | tf_op jit(solution)/shard_map/cthld,clhde->cthe/dot_general | solution.py:116
  186.4 2.6 %psum.7 = f32[1024]{0:T(1024)S(1)} all-reduce(f32[1024]{0:T(1024)S(1)} %bitcast.71), channel_id=1, replica_groups=mesh['seq'=16,'head'=2] {'head'}, use_global_device_ids=true, to_apply=%region_2.3 | all-reduce | flops 1024 | bytes 8192 | tf_op jit(solution)/shard_map/psum | solution.py:124
  189.0 8.3 %copy.82 = f32[4,256,16,128]{3,2,1,0:T(8,128)S(1)} copy(f32[4,256,16,128]{3,1,2,0:T(8,128)} %get-tuple-element.24) | data formatting | bytes 16777216 | tf_op jit(solution)/shard_map/add | solution.py:120
  197.2 0.0 copy-done.11
  197.2 4.7 %fusion.8 = bf16[1024,16,128]{2,1,0:T(8,128)(2,1)} fusion(f32[4,256,16,128]{3,2,1,0:T(8,128)S(1)} %copy.82, f32[16,128]{1,0:T(8,128)S(1)} %copy-done.11, f32[1024]{0:T(1024)S(1)} %add_rsqrt_fusion), kind=kLoop, calls=%fused_computation.14 | loop fusion | flops 6291456 | bytes 12595200 | tf_op jit(solution)/shard_map/convert_element_type | solution.py:126
  (16 shorter events, 0.1 us)
Async XLA Ops:
  0.0 1.2 slice-start
  0.0 1.5 slice-start.1
  1.5 5.5 %copy-start = (bf16[1024,16,128]{2,1,0:T(8,128)(2,1)S(1)}, bf16[1024,16,128]{2,1,0:T(8,128)(2,1)}, u32[]{:S(2)}) copy-start(bf16[1024,16,128]{2,1,0:T(8,128)(2,1)} %param.6) | copy-start | bytes 12582916
  1.5 5.5 %copy-start.2 = (bf16[1024,16,128]{2,1,0:T(8,128)(2,1)S(1)}, bf16[1024,16,128]{2,1,0:T(8,128)(2,1)}, u32[]{:S(2)}) copy-start(bf16[1024,16,128]{2,1,0:T(8,128)(2,1)} %param.7) | copy-start | bytes 12582916
  3.6 88.6 %collective-permute-start.2 = (bf16[2,256,16,128]{3,1,2,0:T(8,128)(2,1)}, bf16[2,256,16,128]{3,1,2,0:T(8,128)(2,1)}, u32[]{:S(2)}, u32[]{:S(2)}) collective-permute-start(bf16[2,256,16,128]{3,1,2,0:T(8,128)(2,1)} %pad_maximum_fusion.1), channel_id=1, source_target_pairs={{0,2},{2,4},{4,6},{6,8},{8,10},{10,12},{12,14},{14,16},{16,18},{18... | collective-permute-start | bytes 6291464 | tf_op jit(solution)/shard_map/ppermute | solution.py:17
  11.1 53.5 %copy-start.4 = (bf16[16,128,128]{2,1,0:T(8,128)(2,1)}, bf16[16,128,128]{2,1,0:T(8,128)(2,1)S(1)}, u32[]{:S(2)}) copy-start(bf16[16,128,128]{2,1,0:T(8,128)(2,1)S(1)} %get-tuple-element.21) | copy-start | bytes 1572868
  11.1 53.5 %collective-permute-start = (bf16[16,128,128]{2,1,0:T(8,128)(2,1)S(1)}, bf16[16,128,128]{2,1,0:T(8,128)(2,1)S(1)}, u32[]{:S(2)}, u32[]{:S(2)}) collective-permute-start(bf16[16,128,128]{2,1,0:T(8,128)(2,1)S(1)} %get-tuple-element.21), channel_id=1, source_target_pairs={{0,2},{2,0},{4,6},{6,4},{8,10},{10,8},{12,14},{14,12},{16,18},{18,... | collective-permute-start | bytes 1572872 | tf_op jit(solution)/shard_map/ppermute | solution.py:75
  25.2 3.3 %copy-start.10 = (f32[7,16,1024]{2,1,0:T(8,128)S(1)}, f32[7,16,1024]{2,1,0:T(8,128)}, u32[]{:S(2)}) copy-start(f32[7,16,1024]{2,1,0:T(8,128)} %param.8) | copy-start | bytes 1376260
  28.6 36.1 %copy-start.8 = (f32[7,2,4,8,256]{4,3,1,2,0:T(8,128)}, f32[7,2,4,8,256]{4,3,1,2,0:T(8,128)S(1)}, u32[]{:S(2)}) copy-start(f32[7,2,4,8,256]{4,3,1,2,0:T(8,128)S(1)} %copy.120) | copy-start | bytes 1376260
  64.7 16.4 %copy-start.6 = (bf16[16,128,128]{2,1,0:T(8,128)(2,1)}, bf16[16,128,128]{2,1,0:T(8,128)(2,1)S(1)}, u32[]{:S(2)}) copy-start(bf16[16,128,128]{2,1,0:T(8,128)(2,1)S(1)} %collective-permute-done) | copy-start | bytes 1572868
  65.7 15.4 %copy-start.1 = (bf16[1024,16,128]{2,1,0:T(8,128)(2,1)S(1)}, bf16[1024,16,128]{2,1,0:T(8,128)(2,1)}, u32[]{:S(2)}) copy-start(bf16[1024,16,128]{2,1,0:T(8,128)(2,1)} %param.6) | copy-start | bytes 12582916
  65.7 25.4 %collective-permute-start.1 = (bf16[16,128,128]{2,1,0:T(8,128)(2,1)}, bf16[16,128,128]{2,1,0:T(8,128)(2,1)}, u32[]{:S(2)}, u32[]{:S(2)}) collective-permute-start(bf16[16,128,128]{2,1,0:T(8,128)(2,1)} %fusion.50), channel_id=1, source_target_pairs={{0,4},{2,6},{4,0},{6,2},{8,12},{10,14},{12,8},{14,10},{16,20},{18,... | collective-permute-start | bytes 1572872 | tf_op jit(solution)/shard_map/ppermute | solution.py:75
  81.1 2.2 %copy-start.3 = (bf16[1024,16,128]{2,1,0:T(8,128)(2,1)S(1)}, bf16[1024,16,128]{2,1,0:T(8,128)(2,1)}, u32[]{:S(2)}) copy-start(bf16[1024,16,128]{2,1,0:T(8,128)(2,1)} %param.7) | copy-start | bytes 12582916
  96.2 9.9 %copy-start.5 = (bf16[16,128,128]{2,1,0:T(8,128)(2,1)S(1)}, bf16[16,128,128]{2,1,0:T(8,128)(2,1)}, u32[]{:S(2)}) copy-start(bf16[16,128,128]{2,1,0:T(8,128)(2,1)} %copy-done.4) | copy-start | bytes 1572868
  96.2 9.9 %copy-start.7 = (bf16[16,128,128]{2,1,0:T(8,128)(2,1)S(1)}, bf16[16,128,128]{2,1,0:T(8,128)(2,1)}, u32[]{:S(2)}) copy-start(bf16[16,128,128]{2,1,0:T(8,128)(2,1)} %copy-done.6) | copy-start | bytes 1572868
  107.1 13.0 %collective-permute-start.3 = (bf16[16,128,128]{2,1,0:T(8,128)(2,1)}, bf16[16,128,128]{2,1,0:T(8,128)(2,1)}, u32[]{:S(2)}, u32[]{:S(2)}) collective-permute-start(bf16[16,128,128]{2,1,0:T(8,128)(2,1)} %fusion.57), channel_id=1, source_target_pairs={{0,8},{2,10},{4,12},{6,14},{8,0},{10,2},{12,4},{14,6},{16,24},{18,... | collective-permute-start | bytes 1572872 | tf_op jit(solution)/shard_map/ppermute | solution.py:75
  121.7 27.8 %collective-permute-start.4 = (bf16[16,128,128]{2,1,0:T(8,128)(2,1)S(1)}, bf16[16,128,128]{2,1,0:T(8,128)(2,1)S(1)}, u32[]{:S(2)}, u32[]{:S(2)}) collective-permute-start(bf16[16,128,128]{2,1,0:T(8,128)(2,1)S(1)} %get-tuple-element.16), channel_id=1, source_target_pairs={{0,16},{2,18},{4,20},{6,22},{8,24},{10,26},{12,28},{14,30},{1,17},... | collective-permute-start | bytes 1572872 | tf_op jit(solution)/shard_map/ppermute | solution.py:75
  157.2 9.3 %copy-start.9 = (bf16[1,1,16,128,128]{3,4,1,2,0:T(8,128)(2,1)S(1)}, bf16[1,1,16,128,128]{3,4,1,2,0:T(8,128)(2,1)}, u32[]{:S(2)}) copy-start(bf16[1,1,16,128,128]{3,4,1,2,0:T(8,128)(2,1)} %copy.77) | copy-start | bytes 1572868
  189.0 8.3 %copy-start.11 = (f32[16,128]{1,0:T(8,128)S(1)}, f32[16,128]{1,0:T(8,128)}, u32[]{:S(2)}) copy-start(f32[16,128]{1,0:T(8,128)} %param.9) | copy-start | bytes 24580

commit v5 on v4

--- a/solution.py
+++ b/solution.py
@@ -32,8 +32,6 @@
     arrived = shifted(last_pair, "seq", 1)
     halo_keys = arrived[0]
     halo_values = arrived[1]
-    prev_keys = jnp.concatenate([halo_keys[None], key_blocks[:-1]], 0)
-    prev_values = jnp.concatenate([halo_values[None], value_blocks[:-1]], 0)
     positions = jnp.arange(STRETCH)
     causal = positions[:, None] >= positions[None, :]
     own_scores = (
@@ -42,14 +40,35 @@
     )
     own_scores = jnp.where(causal, own_scores, 0.0).astype(jnp.bfloat16)
     prev_scores = (
-        jnp.einsum("cthd,cuhd->chtu", query_blocks, prev_keys, preferred_element_type=jnp.float32)
+        jnp.concatenate(
+            [
+                jnp.einsum(
+                    "thd,uhd->htu", query_blocks[0], halo_keys, preferred_element_type=jnp.float32
+                )[None],
+                jnp.einsum(
+                    "cthd,cuhd->chtu",
+                    query_blocks[1:],
+                    key_blocks[:-1],
+                    preferred_element_type=jnp.float32,
+                ),
+            ],
+            0,
+        )
         * score_scale
     ).astype(jnp.bfloat16)
     own_part = jnp.einsum(
         "chtu,cuhd->cthd", own_scores, value_blocks, preferred_element_type=jnp.float32
     )
-    prev_part = jnp.einsum(
-        "chtu,cuhd->cthd", prev_scores, prev_values, preferred_element_type=jnp.float32
+    prev_part = jnp.concatenate(
+        [
+            jnp.einsum(
+                "htu,uhd->thd", prev_scores[0], halo_values, preferred_element_type=jnp.float32
+            )[None],
+            jnp.einsum(
+                "chtu,cuhd->cthd", prev_scores[1:], value_blocks[:-1], preferred_element_type=jnp.float32
+            ),
+        ],
+        0,
     )
     block_states = jnp.einsum(
         "cuhd,cuhe->chde", key_blocks, value_blocks, preferred_element_type=jnp.float32

time: 203 us -> 196 us (0.966)
  waiting for transfers between devices: 66.5 us -> 47.1 us
  other arithmetic: 40.2 us -> 50.3 us
  matrix products: 48.7 us -> 54.3 us
  local copies, waits for them, and re-layouts: 35.5 us -> 31.4 us
    ppermute x4, waiting for transfers between devices: 66.5 us -> 47.1 us  [on_device(): lax.ppermute(running.astype(jnp.bfloat16), 'seq', pairs).astype(jnp.float32)]
    slice x6 -> x4, local copies, waits for them, and re-layouts: 11 us -> 3.46 us  [the longest x1 2.2 us: on_device(): value_blocks[:-1]]
    convert_element_type x0 -> x1, other arithmetic: none -> 6.02 us  [on_device(): prev_scores = (jnp.concatenate([jnp.einsum('thd,uhd->htu', query_blocks[0...]
    concatenate x0 -> x1, other arithmetic: none -> 5.97 us  [on_device(): jnp.concatenate([jnp.einsum('htu,uhd->thd', prev_scores[0], halo_values,...]
    dot_general x1 -> x4, matrix products: 9.89 us -> 15.7 us  [the longest x1 6.29 us: on_device(): jnp.einsum('cthd,cuhd->chtu', query_blocks[1:], key_blocks[:-1], preferre...]
  transfers between devices with their start and end apart: 5 -> 5, of which waited for: 3 -> 4; matrix products, arithmetic and copies ran while one was open for 26% -> 29% of each run, Pallas kernels for 0% -> 0%
where the time goes in v5:
time: 196 us; the launch traced here: 195 us
  matrix products  54.3 us (28%)
  other arithmetic  50.3 us (26%)
  waiting for transfers between devices  47.1 us (24%)
  local copies, waits for them, and re-layouts  31.4 us (16%)
  starting transfers between devices  8.56 us (4%)
  blocking collectives  2.6 us (1%)
    ppermute x4, waiting for transfers between devices, on_device(): lax.ppermute(running.astype(jnp.bfloat16), 'seq', pairs).astype(jnp.float32)  47.1 us
    dot_general x1, matrix products, on_device(): jnp.einsum('cthld,clhde->cthe', scaled, far_states, preferred_element_typ...  19.7 us
    convert_element_type x1, other arithmetic, on_device(): scaled = (query_blocks[:, :, :, None, :] * weight_blocks[:, :, :, 2:, Non...  14.8 us
    dot_general x1, matrix products, on_device(): jnp.einsum('chtu,cuhd->cthd', own_scores, value_blocks, preferred_element...  12.8 us
    another operation x2, other arithmetic  9.42 us
    add x1, local copies, waits for them, and re-layouts, on_device(): weight_blocks[:, :, :, 0:1] * own_part  8.25 us
    dot_general x1, matrix products, on_device(): jnp.einsum('cthd,cuhd->chtu', query_blocks[1:], key_blocks[:-1], preferre...  6.29 us
    convert_element_type x1, other arithmetic, on_device(): prev_scores = (jnp.concatenate([jnp.einsum('thd,uhd->htu', query_blocks[0...  6.02 us
  transfers between devices with their start and end apart: 5, of which 4 were waited for; matrix products, arithmetic and copies ran while one was open for 29% of the time, Pallas kernels for 0%

profile of v5, /device:TPU:25, one launch (start us, length us, event | category | flops | bytes accessed | tf_op | source)
XLA Modules:
  0.0 194.5 jit_solution(9937919238641872479)
XLA Ops:
  0.0 1.2 slice-done
  1.2 0.3 slice-done.1
  1.5 0.5 copy_bitcast_fusion
  2.1 1.5 pad_maximum_fusion.2
  3.6 3.4 %collective-permute-start.2 = (bf16[2,256,16,128]{3,1,2,0:T(8,128)(2,1)}, bf16[2,256,16,128]{3,1,2,0:T(8,128)(2,1)}, u32[]{:S(2)}, u32[]{:S(2)}) collective-permute-start(bf16[2,256,16,128]{3,1,2,0:T(8,128)(2,1)} %pad_maximum_fusion.2), channel_id=1, source_target_pairs={{0,2},{2,4},{4,6},{6,8},{8,10},{10,12},{12,14},{14,16},{16,18},{18... | collective-permute-start | bytes 6291464 | tf_op jit(solution)/shard_map/ppermute | solution.py:17
  7.0 0.0 copy-done.2
  7.0 0.0 copy-done.4
  7.0 0.0 copy-start.14
  7.0 0.0 copy-start
  7.0 4.1 %fusion.51 = (bf16[16,128,128]{2,1,0:T(8,128)(2,1)S(1)}, f32[4,16,128,128]{3,2,1,0:T(8,128)}) fusion(bf16[4,256,16,128]{3,2,1,0:T(8,128)(2,1)S(1)} %bitcast.83, bf16[4,256,16,128]{3,2,1,0:T(8,128)(2,1)S(1)} %bitcast.81), kind=kOutput, calls=%fused_computation.73 | convolution fusion | flops 537657344 | bytes 13107200 | tf_op jit(solution)/shard_map/cuhd,cuhe->chde/dot_general | solution.py:73
  11.1 0.0 copy-start.7
  11.1 1.3 collective-permute-start
  12.4 0.0 copy-done.14
  12.5 0.2 copy.62
  12.7 0.0 copy-done
  12.7 4.4 %copy.61 = f32[4,256,16,128]{3,1,2,0:T(8,128)} copy(bf16[4,256,16,128]{3,2,1,0:T(8,128)(2,1)S(1)} %bitcast.79) | data formatting | bytes 12582912 | tf_op jit(solution)/shard_map/convert_element_type | solution.py:83
  17.1 12.8 %fusion.20 = f32[4,256,16,128]{3,1,2,0:T(8,128)} fusion(bf16[4,256,16,128]{3,2,1,0:T(8,128)(2,1)} %bitcast.82, pred[256,256]{1,0:T(8,128)(4,1)S(1)} %iota_compare_fusion, bf16[4,256,16,128]{3,2,1,0:T(8,128)(2,1)} %bitcast.78, bf16[4,256,16,128]{3,2,1,0:T(8,128)(2,1)} %bitcast.80), kind=kOutput, calls=%fused_computation.27 | convolution fusion | flops 2160066560 | bytes 21037056 | tf_op jit(solution)/shard_map/chtu,cuhd->cthd/dot_general | solution.py:59
  29.9 14.8 %multiply_convert_fusion = bf16[4,256,16,5,128]{4,1,3,2,0:T(8,128)(2,1)} fusion(f32[4,256,16,5]{1,3,2,0:T(8,128)S(1)} %copy.62, f32[4,256,16,128]{3,1,2,0:T(8,128)} %copy.61), kind=kLoop, calls=%fused_computation | loop fusion | flops 31457280 | bytes 29687808 | tf_op jit(solution)/shard_map/convert_element_type | solution.py:84
  44.7 0.0 copy-done.1
  44.7 0.0 copy-start.3
  44.7 0.2 slice.61
  44.9 0.5 slice.62
  45.5 1.4 copy-done.3
  46.9 0.5 slice.64
  47.4 1.6 copy-done.5
  49.1 2.2 %slice.68 = bf16[768,16,128]{2,1,0:T(8,128)(2,1)} slice(bf16[1024,16,128]{2,1,0:T(8,128)(2,1)S(1)} %copy-done.5), slice={[0:768], [0:16], [0:128]} | slice | bytes 6291456 | tf_op jit(solution)/shard_map/slice | solution.py:68
  51.3 2.1 %fusion.45 = bf16[1,1,16,128,128]{4,3,2,1,0:T(8,128)(2,1)} fusion(f32[4,16,128,128]{3,2,1,0:T(8,128)} %get-tuple-element.20), kind=kLoop, calls=%fused_computation.60 | loop fusion | bytes 1048576 | tf_op jit(solution)/shard_map/convert.6
  53.4 11.2 %collective-permute-done = bf16[16,128,128]{2,1,0:T(8,128)(2,1)S(1)} collective-permute-done((bf16[16,128,128]{2,1,0:T(8,128)(2,1)S(1)}, bf16[16,128,128]{2,1,0:T(8,128)(2,1)S(1)}, u32[]{:S(2)}, u32[]{:S(2)}) %collective-permute-start) | collective-permute-done | bytes 524320 | tf_op jit(solution)/shard_map/ppermute | solution.py:94
  64.6 0.0 copy-done.7
  64.6 0.1 fusion.39
  64.8 2.2 %collective-permute-start.1 = (bf16[16,128,128]{2,1,0:T(8,128)(2,1)S(1)}, bf16[16,128,128]{2,1,0:T(8,128)(2,1)S(1)}, u32[]{:S(2)}, u32[]{:S(2)}) collective-permute-start(bf16[16,128,128]{2,1,0:T(8,128)(2,1)S(1)} %fusion.39), channel_id=1, source_target_pairs={{0,4},{2,6},{4,0},{6,2},{8,12},{10,14},{12,8},{14,10},{16,20},{18,... | collective-permute-start | bytes 1572872 | tf_op jit(solution)/shard_map/ppermute | solution.py:94
  67.0 6.3 %fusion.25 = f32[3,16,256,256]{3,2,1,0:T(8,128)} fusion(bf16[3,256,16,128]{3,2,1,0:T(8,128)(2,1)S(1)} %bitcast.77, bf16[3,256,16,128]{3,2,1,0:T(8,128)(2,1)S(1)} %bitcast.76), kind=kOutput, calls=%fused_computation.30 | convolution fusion | flops 805306368 | bytes 18874368 | tf_op jit(solution)/shard_map/cthd,cuhd->chtu/dot_general | solution.py:48
  73.3 0.0 copy-done.10
  73.3 4.9 %collective-permute-done.1 = bf16[16,128,128]{2,1,0:T(8,128)(2,1)S(1)} collective-permute-done((bf16[16,128,128]{2,1,0:T(8,128)(2,1)S(1)}, bf16[16,128,128]{2,1,0:T(8,128)(2,1)S(1)}, u32[]{:S(2)}, u32[]{:S(2)}) %collective-permute-start.1) | collective-permute-done | bytes 524320 | tf_op jit(solution)/shard_map/ppermute | solution.py:94
  78.2 0.1 convert_element_type.76
  78.3 0.0 collective-permute-done.2
  78.3 1.9 convolution_bitcast_fusion
  80.3 6.0 %fusion = bf16[4,16,256,256]{3,2,1,0:T(8,128)(2,1)S(1)} fusion(f32[3,16,256,256]{3,2,1,0:T(8,128)} %fusion.25, f32[1,16,256,256]{3,2,1,0:T(8,128)S(1)} %convolution_bitcast_fusion), kind=kLoop, calls=%fused_computation.2 | loop fusion | flops 12582912 | bytes 25165824 | tf_op jit(solution)/shard_map/convert_element_type | solution.py:58
  86.3 4.2 %fusion.28 = f32[3,256,16,128]{3,1,2,0:T(8,128)S(1)} fusion(bf16[4,16,256,256]{3,2,1,0:T(8,128)(2,1)S(1)} %fusion, bf16[3,256,16,128]{3,2,1,0:T(8,128)(2,1)} %bitcast.84), kind=kOutput, calls=%fused_computation.33 | convolution fusion | flops 805306368 | bytes 17825792 | tf_op jit(solution)/shard_map/chtu,cuhd->cthd/dot_general | solution.py:67
  90.5 3.3 %fusion.32 = f32[1,256,16,128]{3,1,2,0:T(8,128)} fusion(bf16[4,16,256,256]{3,2,1,0:T(8,128)(2,1)S(1)} %fusion, bf16[2,256,16,128]{3,1,2,0:T(8,128)(2,1)} %collective-permute-done.2), kind=kOutput, calls=%fused_computation.39 | convolution fusion | flops 268435456 | bytes 5242880 | tf_op jit(solution)/shard_map/htu,uhd->thd/dot_general | solution.py:64
  93.8 6.0 %pad_maximum_fusion = f32[4,256,16,128]{3,1,2,0:T(8,128)} fusion(f32[3,256,16,128]{3,1,2,0:T(8,128)S(1)} %fusion.28, f32[1,256,16,128]{3,1,2,0:T(8,128)} %fusion.32), kind=kLoop, calls=%fused_computation.12 | loop fusion | flops 2097152 | bytes 16777216 | tf_op jit(solution)/shard_map/concatenate | solution.py:62
  99.8 0.0 copy-done.8
  99.8 1.0 fusion.47
  100.8 0.2 collective-permute-start.3
  100.9 0.1 fusion.46
  101.1 1.0 copy.64
  102.1 1.3 copy.63
  103.5 0.1 pad_maximum_fusion.3
  103.6 9.3 %collective-permute-done.3 = bf16[16,128,128]{2,1,0:T(8,128)(2,1)} collective-permute-done((bf16[16,128,128]{2,1,0:T(8,128)(2,1)}, bf16[16,128,128]{2,1,0:T(8,128)(2,1)}, u32[]{:S(2)}, u32[]{:S(2)}) %collective-permute-start.3) | collective-permute-done | bytes 524320 | tf_op jit(solution)/shard_map/ppermute | solution.py:94
  112.9 0.0 copy-done.12
  112.9 1.5 multiply_bitcast_fusion.1
  114.4 1.5 collective-permute-start.4
  116.0 2.0 %fusion.40 = f32[16,128,128]{1,2,0:T(8,128)S(1)} fusion(bf16[2,256,16,128]{3,1,2,0:T(8,128)(2,1)} %collective-permute-done.2), kind=kOutput, calls=%fused_computation.59 | convolution fusion | flops 134217728 | bytes 3145728 | tf_op jit(solution)/shard_map/uhd,uhe->hde/dot_general | solution.py:76
  118.0 2.6 %broadcast_multiply_fusion = f32[4,16,128,128]{2,3,0,1:T(8,128)} fusion(f32[16,128,128]{1,2,0:T(8,128)S(1)} %fusion.40, f32[4]{0:T(128)S(1)} %pad_maximum_fusion.3), kind=kLoop, calls=%fused_computation.38 | loop fusion | flops 1048576 | bytes 5242896 | tf_op jit(solution)/shard_map/mul | solution.py:129
  120.6 21.6 %collective-permute-done.4 = bf16[16,128,128]{2,1,0:T(8,128)(2,1)S(1)} collective-permute-done((bf16[16,128,128]{2,1,0:T(8,128)(2,1)S(1)}, bf16[16,128,128]{2,1,0:T(8,128)(2,1)S(1)}, u32[]{:S(2)}, u32[]{:S(2)}) %collective-permute-start.4) | collective-permute-done | bytes 524320 | tf_op jit(solution)/shard_map/ppermute | solution.py:94
  142.2 0.1 multiply_bitcast_fusion
  142.3 2.2 %pad_maximum_fusion.1 = f32[4,16,128,128]{3,2,1,0:T(8,128)} fusion(f32[1,16,128,128]{3,2,1,0:T(8,128)S(1)} %multiply_bitcast_fusion, f32[1,16,128,128]{3,2,1,0:T(8,128)S(1)} %get-tuple-element.16, f32[1,16,128,128]{3,2,1,0:T(8,128)S(1)} %get-tuple-element.13, f32[1,16,128,128]{3,2,1,0:T(8,128)S(1)} %get-tuple-element.15), kind=kLoop, calls=%fused_computation.19 | loop fusion | flops 3145728 | bytes 8388608 | tf_op jit(solution)/shard_map/stack | solution.py:103
  144.5 5.4 %copy.65 = f32[4,16,128,128]{2,3,0,1:T(8,128)} copy(f32[4,16,128,128]{3,2,1,0:T(8,128)} %pad_maximum_fusion.1) | data formatting | bytes 8388608 | tf_op jit(solution)/shard_map/stack | solution.py:103
  149.9 9.3 %subtract_convert_fusion = bf16[4,4,16,128,128]{3,4,1,2,0:T(8,128)(2,1)} fusion(f32[4,16,128,128]{2,3,0,1:T(8,128)} %broadcast_multiply_fusion, f32[4]{0:T(128)S(1)} %compare_convert_fusion, f32[4,16,128,128]{2,3,0,1:T(8,128)} %copy.65), kind=kLoop, calls=%fused_computation.3 | loop fusion | flops 12582912 | bytes 16777232 | tf_op jit(solution)/shard_map/convert.4
  159.2 19.7 %multiply_reduce_fusion = (f32[4,256]{1,0:T(4,128)S(1)}, f32[4,256,16,128]{3,1,2,0:T(8,128)}) fusion(bf16[4,256,16,5,128]{4,1,3,2,0:T(8,128)(2,1)} %multiply_convert_fusion, bf16[4,4,16,128,128]{3,4,1,2,0:T(8,128)(2,1)} %subtract_convert_fusion, bf16[1,1,16,128,128]{3,4,1,2,0:T(8,128)(2,1)S(1)} %copy-done.13, bf16[1,1,16,128,128]{3,4,1,2,0:T(8,128)(2,1)S(1)} %copy.63, ...), kind=kOutput, calls=%fused_computation.17 | convolution fusion | flops 2712665088 | bytes 55709736 | tf_op jit(solution)/shard_map/cthld,clhde->cthe/dot_general | solution.py:135
  178.9 2.6 %psum.7 = f32[1024]{0:T(1024)S(1)} all-reduce(f32[1024]{0:T(1024)S(1)} %bitcast.88), channel_id=1, replica_groups=mesh['seq'=16,'head'=2] {'head'}, use_global_device_ids=true, to_apply=%region_2.3 | all-reduce | flops 1024 | bytes 8192 | tf_op jit(solution)/shard_map/psum | solution.py:143
  181.5 8.3 %copy.69 = f32[4,256,16,128]{3,2,1,0:T(8,128)S(1)} copy(f32[4,256,16,128]{3,1,2,0:T(8,128)} %get-tuple-element.22) | data formatting | bytes 16777216 | tf_op jit(solution)/shard_map/add | solution.py:139
  189.8 0.0 copy-done.15
  189.8 4.7 %fusion.9 = bf16[1024,16,128]{2,1,0:T(8,128)(2,1)} fusion(f32[4,256,16,128]{3,2,1,0:T(8,128)S(1)} %copy.69, f32[16,128]{1,0:T(8,128)S(1)} %copy-done.15, f32[1024]{0:T(1024)S(1)} %add_rsqrt_fusion), kind=kLoop, calls=%fused_computation.16 | loop fusion | flops 6291456 | bytes 12595200 | tf_op jit(solution)/shard_map/convert_element_type | solution.py:145
  (27 shorter events, 0.2 us)
Async XLA Ops:
  0.0 1.2 slice-start
  0.0 1.5 slice-start.1
  1.5 5.4 %copy-start.2 = (bf16[1024,16,128]{2,1,0:T(8,128)(2,1)S(1)}, bf16[1024,16,128]{2,1,0:T(8,128)(2,1)}, u32[]{:S(2)}) copy-start(bf16[1024,16,128]{2,1,0:T(8,128)(2,1)} %param.6) | copy-start | bytes 12582916
  1.5 5.4 %copy-start.4 = (bf16[1024,16,128]{2,1,0:T(8,128)(2,1)S(1)}, bf16[1024,16,128]{2,1,0:T(8,128)(2,1)}, u32[]{:S(2)}) copy-start(bf16[1024,16,128]{2,1,0:T(8,128)(2,1)} %param.7) | copy-start | bytes 12582916
  3.6 74.7 %collective-permute-start.2 = (bf16[2,256,16,128]{3,1,2,0:T(8,128)(2,1)}, bf16[2,256,16,128]{3,1,2,0:T(8,128)(2,1)}, u32[]{:S(2)}, u32[]{:S(2)}) collective-permute-start(bf16[2,256,16,128]{3,1,2,0:T(8,128)(2,1)} %pad_maximum_fusion.2), channel_id=1, source_target_pairs={{0,2},{2,4},{4,6},{6,8},{8,10},{10,12},{12,14},{14,16},{16,18},{18... | collective-permute-start | bytes 6291464 | tf_op jit(solution)/shard_map/ppermute | solution.py:17
  7.0 5.5 %copy-start.14 = (f32[7,16,1024]{2,1,0:T(8,128)S(1)}, f32[7,16,1024]{2,1,0:T(8,128)}, u32[]{:S(2)}) copy-start(f32[7,16,1024]{2,1,0:T(8,128)} %param.8) | copy-start | bytes 1376260
  7.0 5.8 %copy-start = (bf16[1024,16,128]{2,1,0:T(8,128)(2,1)S(1)}, bf16[1024,16,128]{2,1,0:T(8,128)(2,1)}, u32[]{:S(2)}) copy-start(bf16[1024,16,128]{2,1,0:T(8,128)(2,1)} %param.5) | copy-start | bytes 12582916
  11.1 53.5 %copy-start.7 = (bf16[16,128,128]{2,1,0:T(8,128)(2,1)}, bf16[16,128,128]{2,1,0:T(8,128)(2,1)S(1)}, u32[]{:S(2)}) copy-start(bf16[16,128,128]{2,1,0:T(8,128)(2,1)S(1)} %get-tuple-element.19) | copy-start | bytes 1572868
  11.1 53.5 %collective-permute-start = (bf16[16,128,128]{2,1,0:T(8,128)(2,1)S(1)}, bf16[16,128,128]{2,1,0:T(8,128)(2,1)S(1)}, u32[]{:S(2)}, u32[]{:S(2)}) collective-permute-start(bf16[16,128,128]{2,1,0:T(8,128)(2,1)S(1)} %get-tuple-element.19), channel_id=1, source_target_pairs={{0,2},{2,0},{4,6},{6,4},{8,10},{10,8},{12,14},{14,12},{16,18},{18,... | collective-permute-start | bytes 1572872 | tf_op jit(solution)/shard_map/ppermute | solution.py:94
  29.9 14.8 %copy-start.1 = (bf16[1024,16,128]{2,1,0:T(8,128)(2,1)S(1)}, bf16[1024,16,128]{2,1,0:T(8,128)(2,1)}, u32[]{:S(2)}) copy-start(bf16[1024,16,128]{2,1,0:T(8,128)(2,1)} %param.5) | copy-start | bytes 12582916
  44.7 2.2 %copy-start.3 = (bf16[1024,16,128]{2,1,0:T(8,128)(2,1)S(1)}, bf16[1024,16,128]{2,1,0:T(8,128)(2,1)}, u32[]{:S(2)}) copy-start(bf16[1024,16,128]{2,1,0:T(8,128)(2,1)} %param.6) | copy-start | bytes 12582916
  46.9 2.2 %copy-start.5 = (bf16[1024,16,128]{2,1,0:T(8,128)(2,1)S(1)}, bf16[1024,16,128]{2,1,0:T(8,128)(2,1)}, u32[]{:S(2)}) copy-start(bf16[1024,16,128]{2,1,0:T(8,128)(2,1)} %param.7) | copy-start | bytes 12582916
  64.6 8.7 %copy-start.10 = (bf16[16,128,128]{2,1,0:T(8,128)(2,1)}, bf16[16,128,128]{2,1,0:T(8,128)(2,1)S(1)}, u32[]{:S(2)}) copy-start(bf16[16,128,128]{2,1,0:T(8,128)(2,1)S(1)} %collective-permute-done) | copy-start | bytes 1572868
  64.8 13.4 %collective-permute-start.1 = (bf16[16,128,128]{2,1,0:T(8,128)(2,1)S(1)}, bf16[16,128,128]{2,1,0:T(8,128)(2,1)S(1)}, u32[]{:S(2)}, u32[]{:S(2)}) collective-permute-start(bf16[16,128,128]{2,1,0:T(8,128)(2,1)S(1)} %fusion.39), channel_id=1, source_target_pairs={{0,4},{2,6},{4,0},{6,2},{8,12},{10,14},{12,8},{14,10},{16,20},{18,... | collective-permute-start | bytes 1572872 | tf_op jit(solution)/shard_map/ppermute | solution.py:94
  93.8 6.0 %copy-start.8 = (bf16[16,128,128]{2,1,0:T(8,128)(2,1)S(1)}, bf16[16,128,128]{2,1,0:T(8,128)(2,1)}, u32[]{:S(2)}) copy-start(bf16[16,128,128]{2,1,0:T(8,128)(2,1)} %copy-done.7) | copy-start | bytes 1572868
  93.8 6.0 %copy-start.11 = (bf16[16,128,128]{2,1,0:T(8,128)(2,1)S(1)}, bf16[16,128,128]{2,1,0:T(8,128)(2,1)}, u32[]{:S(2)}) copy-start(bf16[16,128,128]{2,1,0:T(8,128)(2,1)} %copy-done.10) | copy-start | bytes 1572868
  93.8 7.2 %copy-start.6 = (f32[4,16,128,128]{3,2,1,0:T(8,128)S(1)}, f32[4,16,128,128]{3,2,1,0:T(8,128)}, u32[]{:S(2)}) copy-start(f32[4,16,128,128]{3,2,1,0:T(8,128)} %get-tuple-element.20) | copy-start | bytes 12582916
  99.8 13.1 %copy-start.9 = (bf16[16,128,128]{2,1,0:T(8,128)(2,1)S(1)}, bf16[16,128,128]{2,1,0:T(8,128)(2,1)}, u32[]{:S(2)}) copy-start(bf16[16,128,128]{2,1,0:T(8,128)(2,1)} %copy-done.7) | copy-start | bytes 1572868
  99.8 13.1 %copy-start.12 = (bf16[16,128,128]{2,1,0:T(8,128)(2,1)S(1)}, bf16[16,128,128]{2,1,0:T(8,128)(2,1)}, u32[]{:S(2)}) copy-start(bf16[16,128,128]{2,1,0:T(8,128)(2,1)} %copy-done.10) | copy-start | bytes 1572868
  100.8 12.1 %collective-permute-start.3 = (bf16[16,128,128]{2,1,0:T(8,128)(2,1)}, bf16[16,128,128]{2,1,0:T(8,128)(2,1)}, u32[]{:S(2)}, u32[]{:S(2)}) collective-permute-start(bf16[16,128,128]{2,1,0:T(8,128)(2,1)} %fusion.47), channel_id=1, source_target_pairs={{0,8},{2,10},{4,12},{6,14},{8,0},{10,2},{12,4},{14,6},{16,24},{18,... | collective-permute-start | bytes 1572872 | tf_op jit(solution)/shard_map/ppermute | solution.py:94
  114.4 27.8 %collective-permute-start.4 = (bf16[16,128,128]{2,1,0:T(8,128)(2,1)S(1)}, bf16[16,128,128]{2,1,0:T(8,128)(2,1)S(1)}, u32[]{:S(2)}, u32[]{:S(2)}) collective-permute-start(bf16[16,128,128]{2,1,0:T(8,128)(2,1)S(1)} %get-tuple-element.14), channel_id=1, source_target_pairs={{0,16},{2,18},{4,20},{6,22},{8,24},{10,26},{12,28},{14,30},{1,17},... | collective-permute-start | bytes 1572872 | tf_op jit(solution)/shard_map/ppermute | solution.py:94
  149.9 9.3 %copy-start.13 = (bf16[1,1,16,128,128]{3,4,1,2,0:T(8,128)(2,1)S(1)}, bf16[1,1,16,128,128]{3,4,1,2,0:T(8,128)(2,1)}, u32[]{:S(2)}) copy-start(bf16[1,1,16,128,128]{3,4,1,2,0:T(8,128)(2,1)} %copy.64) | copy-start | bytes 1572868
  181.5 8.3 %copy-start.15 = (f32[16,128]{1,0:T(8,128)S(1)}, f32[16,128]{1,0:T(8,128)}, u32[]{:S(2)}) copy-start(f32[16,128]{1,0:T(8,128)} %param.9) | copy-start | bytes 24580
